TPU v7x, 32 devices: a whole 2x2x4 slice. The times are simulated.
32 devices in a mesh: groups: 2 (over y), imp: 8 (over z, x), adv: 2 (over core).
Axes of the slice: x: 2, y: 2, z: 4, core: 2. Of those that a mesh axis runs over, the one named last changes fastest.
Arguments:
- imp_emb: bfloat16 [4096, 256], P(('groups', 'imp')), parts along dimension 0, may hold values from -6 to 6
- adv_emb: bfloat16 [8192, 256], P(('groups', 'imp', 'adv')), parts along dimension 0, may hold values from -6 to 6
- allowances: int32 [8192], P(('groups', 'imp', 'adv')), parts along dimension 0, may hold values from 1024 to 16383
- eligible_slots: int32 [32, 8], P(('groups', 'imp', 'adv')), parts along dimension 0, may hold values from -1 to 3, as said below
Outputs:
- prices: float32 [4096], P(('groups', 'imp')), parts along dimension 0
- utilities: float32 [8192], P(('groups', 'imp', 'adv')), parts along dimension 0
There are 2 independent parts, one for each index of `groups`. A program takes and returns all parts, laid end to end along the dimension named above; each array names one. Nothing has to cross between parts.
Inputs may be any that keep to these rules, and one draw needn't show every extreme that they name: eligible_slots[d, i] is -1 or k * 2 + m with k < 2 and m < 2; every advertiser block is eligible with at least one impression block.
All inputs are finite; a program needn't handle non-finite values.
Results may differ from a plain program's by a relative error of at most 0.00081.
Values may be sent and summed in bfloat16 or wider, within the bound.
No kernel may reach another device: no remote copies, remote signals or barrier semaphores. Data moves between devices by JAX's collectives and lax.ppermute only.
A program may use at most 128 MiB of HBM per device.

v0:
```python
import math

import jax
import jax.numpy as jnp
from jax import lax
from jax.sharding import PartitionSpec as P

BLK = 128
EMB = 256
IB_DEV = 2
ITERS = 2


def local(imp_emb, adv_emb, allowances, eligible_slots):
    slot_count = eligible_slots.shape[1]
    adv_blocks = adv_emb.shape[0] // BLK
    slot_codes = eligible_slots[0]
    is_live = slot_codes >= 0
    clamped = jnp.maximum(slot_codes, 0)
    adv_pick = clamped // IB_DEV
    imp_pick = clamped % IB_DEV
    wanted = jnp.where(is_live, imp_pick, -1)
    cached = []

    def asked_blocks():
        if not cached:
            cached.append(lax.all_to_all(wanted, "imp", split_axis=0, concat_axis=0, tiled=True))
        return cached[0]

    adv_rows = jnp.take(adv_emb.reshape(adv_blocks, BLK, EMB), adv_pick, axis=0)
    score_scale = 1.0 / math.sqrt(EMB)
    asked = asked_blocks()
    home_slabs = imp_emb.reshape(IB_DEV, BLK, EMB)
    chosen = jnp.take(home_slabs, jnp.maximum(asked, 0), axis=0)
    outgoing = jnp.where((asked >= 0)[:, None, None], chosen, jnp.zeros_like(chosen))
    scores = (
        jnp.einsum(
            "nae,nbe->nab",
            adv_rows,
            lax.all_to_all(outgoing, "imp", split_axis=0, concat_axis=0, tiled=True),
            preferred_element_type=jnp.float32,
        )
        * score_scale
    )
    value_tiles = jnp.where(is_live[:, None, None], jax.nn.softplus(scores), 0.0).astype(
        jnp.bfloat16
    )
    highest = lax.Precision.HIGHEST
    spend_rows = allowances.astype(jnp.float32).reshape(adv_blocks, BLK) / 1024.0
    block_ids = jnp.arange(adv_blocks, dtype=jnp.int32)
    picker = (adv_pick[:, None] == block_ids[None, :]).astype(jnp.float32)
    live_picker = picker * is_live[:, None].astype(jnp.float32)
    row_totals = jnp.sum(value_tiles, axis=2, dtype=jnp.float32)
    value_sums = jnp.einsum("nk,na->ka", live_picker, row_totals, precision=highest)
    slot_spend = jnp.einsum("nk,ka->na", live_picker, spend_rows, precision=highest)
    slot_sums = jnp.einsum("nk,ka->na", picker, value_sums, precision=highest)
    bid_tiles = (slot_spend / slot_sums)[:, :, None] * value_tiles
    home_ids = jnp.arange(IB_DEV, dtype=jnp.int32)
    utility = jnp.zeros((adv_blocks, BLK), jnp.float32)
    home_prices = jnp.zeros((IB_DEV, BLK), jnp.float32)
    slot_prices = jnp.zeros((slot_count, BLK), jnp.float32)
    for round_index in range(ITERS + 1):
        totals = jnp.sum(bid_tiles, axis=1)
        asked = asked_blocks()
        asked_picker = (asked[:, None] == home_ids[None, :]).astype(jnp.float32)
        arrived = lax.all_to_all(totals, "imp", split_axis=0, concat_axis=0, tiled=True)
        partial_value = jnp.einsum("ok,oj->kj", asked_picker, arrived, precision=highest)
        home_prices = lax.psum(partial_value, "adv")
        if round_index < ITERS:
            returned = jnp.einsum("ok,kj->oj", asked_picker, home_prices, precision=highest)
            slot_prices = lax.all_to_all(returned, "imp", split_axis=0, concat_axis=0, tiled=True)
        if round_index < ITERS:
            divisor = jnp.where(is_live[:, None], slot_prices, 1.0)
            shares = bid_tiles / divisor[:, None, :]
            earned = value_tiles * shares
            utility = jnp.einsum(
                "nk,na->ka", live_picker, jnp.sum(earned, axis=2), precision=highest
            )
            slot_utility = jnp.einsum("nk,ka->na", picker, utility, precision=highest)
            bid_tiles = (slot_spend / slot_utility)[:, :, None] * earned
    return (home_prices.reshape(IB_DEV * BLK), utility.reshape(adv_blocks * BLK))


def solution(mesh):
    return jax.shard_map(
        local,
        mesh=mesh,
        in_specs=(
            P(("groups", "imp"), None),
            P(("groups", "imp", "adv"), None),
            P(("groups", "imp", "adv")),
            P(("groups", "imp", "adv"), None),
        ),
        out_specs=(P(("groups", "imp")), P(("groups", "imp", "adv"))),
        check_vma=False,
    )
```

profile of v0, /device:TPU:0, one launch (start us, length us, event | category | flops | bytes accessed | tf_op | source)
XLA Modules:
  0.0 92.8 jit_solution(4082183980826670276)
XLA Ops:
  0.6 0.0 copy-start
  0.6 0.7 bitcast_select_fusion.1
  1.3 0.1 copy.10
  1.4 13.6 %all_to_all.65 = s32[8,1,1]{2,1,0:T(1,128)S(1)} all-to-all(s32[8,1,1]{2,1,0:T(1,128)S(1)} %copy.10), channel_id=1, replica_groups=mesh['groups'=2,'imp'=8,'adv'=2] {'imp'}, dimensions={0} | all-to-all | bytes 64 | tf_op jit(solution)/shard_map/all_to_all | solution.py:27
  15.0 0.2 reduce
  15.3 0.1 copy.11
  15.3 0.0 copy-done
  15.4 0.6 gather_fusion.1
  15.9 0.9 %select_select_fusion = bf16[8,128,256]{2,1,0:T(8,128)(2,1)} fusion(bf16[8,128,256]{2,1,0:T(8,128)(2,1)S(1)} %gather_fusion.1, pred[8]{0:T(512)(128)(4,1)S(1)} %broadcast_compare_fusion, pred[8]{0:T(512)(128)(4,1)S(1)} %compare_bitcast_fusion), kind=kLoop, calls=%fused_computation.15 | loop fusion | flops 524288 | bytes 1048592 | tf_op jit(solution)/shard_map/jit(_where)/select_n | solution.py:35
  16.9 0.0 copy-start.3
  16.9 0.0 copy-start.1
  16.9 3.6 %all-to-all-start.1 = ((bf16[8,128,256]{2,1,0:T(8,128)(2,1)}), bf16[8,128,256]{2,1,0:T(8,128)(2,1)S(1)}, u32[]{:S(2)}, u32[]{:S(2)}) async-start(bf16[8,128,256]{2,1,0:T(8,128)(2,1)} %select_select_fusion), calls=%async_computation.1 | async-start | bytes 1048576 | tf_op jit(solution)/shard_map/all_to_all | solution.py:40
  20.5 0.0 copy-done.3
  20.6 0.0 copy-done.1
  20.6 0.6 gather_fusion
  21.2 0.0 copy-start.2
  21.2 0.7 copy-done.2
  21.9 0.2 fusion.13
  22.1 11.7 %all-to-all-done.1 = bf16[8,128,256]{2,1,0:T(8,128)(2,1)S(1)} async-done(((bf16[8,128,256]{2,1,0:T(8,128)(2,1)}), bf16[8,128,256]{2,1,0:T(8,128)(2,1)S(1)}, u32[]{:S(2)}, u32[]{:S(2)}) %all-to-all-start.1) | async-done | bytes 524320 | tf_op jit(solution)/shard_map/all_to_all | solution.py:40
  33.8 0.4 fusion.6
  34.1 0.4 convert_reduce_fusion
  34.5 0.3 fusion.11
  34.8 0.2 convolution_divide_fusion.2
  35.0 0.2 fusion.1
  35.2 10.0 %all_to_all.66 = f32[8,1,128]{2,1,0:T(1,128)S(1)} all-to-all(f32[8,1,128]{2,1,0:T(1,128)S(1)} %bitcast.59), channel_id=1, replica_groups=mesh['groups'=2,'imp'=8,'adv'=2] {'imp'}, dimensions={0} | all-to-all | bytes 8192 | tf_op jit(solution)/shard_map/all_to_all | solution.py:66
  45.2 0.3 fusion.18
  45.4 2.5 %psum.21 = f32[2,128]{1,0:T(2,128)S(1)} all-reduce(f32[2,128]{1,0:T(2,128)S(1)} %fusion.18), channel_id=1, replica_groups=mesh['groups'=2,'imp'=8,'adv'=2] {'adv'}, use_global_device_ids=true, to_apply=%region_2.4 | all-reduce | flops 256 | bytes 2048 | tf_op jit(solution)/shard_map/psum | solution.py:68
  47.9 0.2 fusion.17
  48.1 8.9 %all_to_all.67 = f32[8,1,128]{2,1,0:T(1,128)S(1)} all-to-all(f32[8,1,128]{2,1,0:T(1,128)S(1)} %bitcast.63), channel_id=1, replica_groups=mesh['groups'=2,'imp'=8,'adv'=2] {'imp'}, dimensions={0} | all-to-all | bytes 8192 | tf_op jit(solution)/shard_map/all_to_all | solution.py:71
  56.9 0.1 broadcast_select_fusion.1
  57.0 0.4 fusion.5
  57.4 0.3 fusion.9
  57.7 0.2 convolution_divide_fusion.1
  57.8 0.4 multiply_reduce_fusion.1
  58.2 8.9 %all_to_all.68 = f32[8,1,128]{2,1,0:T(1,128)S(1)} all-to-all(f32[8,1,128]{2,1,0:T(1,128)S(1)} %bitcast.60), channel_id=1, replica_groups=mesh['groups'=2,'imp'=8,'adv'=2] {'imp'}, dimensions={0} | all-to-all | bytes 8192 | tf_op jit(solution)/shard_map/all_to_all | solution.py:66
  67.1 0.3 fusion.16
  67.3 2.5 %psum.22 = f32[2,128]{1,0:T(2,128)S(1)} all-reduce(f32[2,128]{1,0:T(2,128)S(1)} %fusion.16), channel_id=1, replica_groups=mesh['groups'=2,'imp'=8,'adv'=2] {'adv'}, use_global_device_ids=true, to_apply=%region_5.7 | all-reduce | flops 256 | bytes 2048 | tf_op jit(solution)/shard_map/psum | solution.py:68
  69.8 0.2 fusion.15
  70.0 8.9 %all_to_all.69 = f32[8,1,128]{2,1,0:T(1,128)S(1)} all-to-all(f32[8,1,128]{2,1,0:T(1,128)S(1)} %bitcast.65), channel_id=1, replica_groups=mesh['groups'=2,'imp'=8,'adv'=2] {'imp'}, dimensions={0} | all-to-all | bytes 8192 | tf_op jit(solution)/shard_map/all_to_all | solution.py:71
  78.8 0.1 broadcast_select_fusion
  78.9 0.5 fusion.50
  79.4 0.3 fusion.7
  79.7 0.2 convolution_divide_fusion
  79.9 0.4 copy-done.4
  80.2 0.5 multiply_reduce_fusion
  80.7 8.9 %all_to_all.70 = f32[8,1,128]{2,1,0:T(1,128)S(1)} all-to-all(f32[8,1,128]{2,1,0:T(1,128)S(1)} %bitcast.58), channel_id=1, replica_groups=mesh['groups'=2,'imp'=8,'adv'=2] {'imp'}, dimensions={0} | all-to-all | bytes 8192 | tf_op jit(solution)/shard_map/all_to_all | solution.py:66
  89.6 0.3 convolution_bitcast_fusion
  89.8 3.0 %psum.23 = f32[256]{0:T(256)} all-reduce(f32[256]{0:T(256)S(1)} %convolution_bitcast_fusion), channel_id=1, replica_groups=mesh['groups'=2,'imp'=8,'adv'=2] {'adv'}, use_global_device_ids=true, to_apply=%region_8.10 | all-reduce | flops 256 | bytes 2048 | tf_op jit(solution)/shard_map/psum | solution.py:68
  (9 shorter events, 0.1 us)
Async XLA Ops:
  0.6 14.7 %copy-start = (bf16[256,256]{1,0:T(8,128)(2,1)S(1)}, bf16[256,256]{1,0:T(8,128)(2,1)}, u32[]{:S(2)}) copy-start(bf16[256,256]{1,0:T(8,128)(2,1)} %param.6) | copy-start | bytes 393220
  16.9 3.6 %copy-start.3 = (s32[1,8]{1,0:T(1,128)S(1)}, s32[1,8]{1,0:T(1,128)}, u32[]{:S(2)}) copy-start(s32[1,8]{1,0:T(1,128)} %param.9) | copy-start | bytes 100
  16.9 3.7 %copy-start.1 = (bf16[256,256]{1,0:T(8,128)(2,1)S(1)}, bf16[256,256]{1,0:T(8,128)(2,1)}, u32[]{:S(2)}) copy-start(bf16[256,256]{1,0:T(8,128)(2,1)} %param.7) | copy-start | bytes 393220
  16.9 16.9 %all-to-all-start.1 = ((bf16[8,128,256]{2,1,0:T(8,128)(2,1)}), bf16[8,128,256]{2,1,0:T(8,128)(2,1)S(1)}, u32[]{:S(2)}, u32[]{:S(2)}) async-start(bf16[8,128,256]{2,1,0:T(8,128)(2,1)} %select_select_fusion), calls=%async_computation.1 | async-start | bytes 1048576 | tf_op jit(solution)/shard_map/all_to_all | solution.py:40
  21.2 0.7 copy-start.2
  79.7 0.6 copy-start.4
where the time goes:
time: 93.4 us; the launch traced here: 92.8 us
  blocking collectives  66.9 us (72%)
  waiting for transfers between devices  11.7 us (13%)
  other arithmetic  4.45 us (5%)
  starting transfers between devices  3.62 us (4%)
  matrix products  3.02 us (3%)
  local copies, waits for them, and re-layouts  2.4 us (3%)
    all_to_all x3, blocking collectives, local(): lax.all_to_all(totals, 'imp', split_axis=0, concat_axis=0, tiled=True)  27.7 us
    all_to_all x2, blocking collectives, local(): lax.all_to_all(returned, 'imp', split_axis=0, concat_axis=0, tiled=True)  17.7 us
    all_to_all x1, blocking collectives, asked_blocks(): lax.all_to_all(wanted, 'imp', split_axis=0, concat_axis=0, tiled=True)  13.6 us
    all_to_all x1, waiting for transfers between devices, local(): lax.all_to_all(outgoing, 'imp', split_axis=0, concat_axis=0, tiled=True)  11.7 us
    psum x3, blocking collectives, local(): home_prices = lax.psum(partial_value, 'adv')  7.91 us
    all_to_all x1, starting transfers between devices, local(): lax.all_to_all(outgoing, 'imp', split_axis=0, concat_axis=0, tiled=True)  3.62 us
  transfers between devices with their start and end apart: 1, of which 1 were waited for; matrix products, arithmetic and copies ran while one was open for 1% of the time, Pallas kernels for 0%

commit v1 on v0

--- a/solution.py
+++ b/solution.py
@@ -1,17 +1,389 @@
+import functools
 import math
 
 import jax
 import jax.numpy as jnp
 from jax import lax
+from jax.experimental import pallas as pl
+from jax.experimental.pallas import tpu as pltpu
 from jax.sharding import PartitionSpec as P
 
 BLK = 128
 EMB = 256
 IB_DEV = 2
+AB_DEV = 2
 ITERS = 2
-
-
-def local(imp_emb, adv_emb, allowances, eligible_slots):
+HOMES = 8
+WIDE = IB_DEV * BLK
+NOTES = 16
+REP = (2, 4)
+GROUPS = ((0, 2, 4, 6),)
+
+F32 = jnp.float32
+BF16 = jnp.bfloat16
+SMEM = pl.BlockSpec(memory_space=pltpu.SMEM)
+VMEM = pl.BlockSpec(memory_space=pltpu.VMEM)
+LIMIT = 24 << 20
+
+
+def take(refs, *counts):
+    parts = []
+    for n in counts:
+        parts.append(refs[:n])
+        refs = refs[n:]
+    return (*parts, refs)
+
+
+def make_eye():
+    return lax.broadcasted_iota(jnp.int32, (BLK, BLK), 0) == lax.broadcasted_iota(
+        jnp.int32, (BLK, BLK), 1
+    )
+
+
+def softplus(s):
+    e = jnp.exp(-jnp.abs(s))
+    near = e - (e * e) * (0.5 - e * (1.0 / 3.0))
+    return jnp.maximum(s, 0.0) + jnp.where(e < 0.004, near, jnp.log(1.0 + e))
+
+
+def fold(tile):
+    return jnp.sum(tile.reshape(BLK // 8, 8, BLK), axis=0)
+
+
+def slot_of(codes, owner, home):
+    code = codes[owner][lax.bitwise_xor(lax.axis_index("imp"), home)]
+    clamped = jnp.maximum(code, 0)
+    return code >= 0, lax.shift_right_logical(clamped, 1), lax.bitwise_and(clamped, 1)
+
+
+def row_block(ref, index):
+    return ref[pl.ds(pl.multiple_of(index * BLK, BLK), BLK), :]
+
+
+def gather_homes(imp_s, core, own, arrived):
+    imp_s[pl.ds(0, WIDE), :] = own[...]
+    for first, second, ref in arrived:
+        d = jnp.where(core == 0, first, second)
+        imp_s[pl.ds(pl.multiple_of(d * WIDE, WIDE), WIDE), :] = ref[...]
+
+
+def score(lhs, rhs):
+    return lax.dot_general(
+        lhs, rhs, (((1,), (1,)), ((), ())), preferred_element_type=F32
+    ) * (1.0 / math.sqrt(EMB))
+
+
+def value_kernel(count, arrivals, *refs):
+    own = arrivals is not None
+    adv, refs = take(refs, count)
+    eye = make_eye()
+    if own:
+        imp_own, *blocks = refs[: 1 + len(arrivals)]
+        refs = refs[1 + len(arrivals) :]
+        values, spend_out, factor_out, price_out, code_out, imp_s, table, sem, acc, pacc = refs
+    else:
+        imp_s, price_in, *refs = refs
+        values, spend_out, factor_out, price_out, code_out, table, sem, acc, pacc = refs
+    notes = [adv[o][pl.ds(WIDE, NOTES), :].astype(F32) for o in range(count)]
+    for o in range(count):
+        code_out[pl.ds(o, 1), :] = notes[o][2:3, :BLK].astype(jnp.int32)
+    copy = pltpu.make_async_copy(code_out, table, sem)
+    copy.start()
+    if own:
+        core = lax.axis_index("adv")
+        gather_homes(imp_s, core, imp_own, [(*d, r) for d, r in zip(arrivals, blocks)])
+        pacc[...] = jnp.zeros_like(pacc)
+    else:
+        for row in range(HOMES * IB_DEV):
+            pacc[row] = jnp.concatenate(
+                [price_in[pl.ds(row, 1), :], jnp.zeros((7, BLK), F32)], axis=0
+            )
+    for o in range(count):
+        spending = (notes[o][0:1] * 128.0 + notes[o][1:2]) * (1.0 / 1024.0)
+        for k in range(AB_DEV):
+            row = spending[:, k * BLK : (k + 1) * BLK]
+            col = jnp.sum(jnp.where(eye, row, 0.0), axis=1, keepdims=True)
+            spend_out[o * AB_DEV + k] = jnp.broadcast_to(col, (BLK, BLK))
+    copy.wait()
+    codes = [table.at[o] for o in range(count)]
+    acc[...] = jnp.zeros_like(acc)
+
+    def value_body(m, carry):
+        slots = [slot_of(codes, o, m) for o in range(count)]
+        picked = [row_block(adv[o], slots[o][1]) for o in range(count)]
+        if WIDE_DOT:
+            rhs = imp_s[pl.ds(pl.multiple_of(m * WIDE, WIDE), WIDE), :]
+            lhs = jnp.concatenate(picked, axis=0)
+            both = score(lhs, rhs)
+        for o, (live, k, b) in enumerate(slots):
+            if WIDE_DOT:
+                s = both[o * BLK : (o + 1) * BLK]
+                s = jnp.where(b == 0, s[:, :BLK], s[:, BLK:])
+            else:
+                s = score(picked[o], row_block(imp_s, m * IB_DEV + b))
+            v = jnp.where(live, softplus(s), 0.0).astype(BF16)
+            values[o * HOMES + m] = v
+            acc[o * AB_DEV + k] += v.astype(F32)
+        return carry
+
+    lax.fori_loop(0, HOMES, value_body, 0, unroll=max(1, UNROLL_V // count))
+    for r in range(count * AB_DEV):
+        total = jnp.sum(acc[r], axis=1, keepdims=True)
+        factor_out[r] = spend_out[r] / total
+
+    def bid_body(m, carry):
+        for o in range(count):
+            _, k, b = slot_of(codes, o, m)
+            pacc[m * IB_DEV + b] += fold(
+                factor_out[o * AB_DEV + k] * values[o * HOMES + m].astype(F32)
+            )
+        return carry
+
+    lax.fori_loop(0, HOMES, bid_body, 0, unroll=max(1, UNROLL_B // count))
+    for row in range(HOMES * IB_DEV):
+        price_out[pl.ds(row, 1), :] = jnp.sum(pacc[row], axis=0, keepdims=True)
+
+
+def add_prices(parts):
+    rows = []
+    for m in range(HOMES):
+        terms = [ref[pl.ds((m ^ d) * IB_DEV, IB_DEV), :] for d, ref in parts]
+        while len(terms) > 1:
+            terms = [terms[i] + terms[i + 1] for i in range(0, len(terms), 2)]
+        rows.append(terms[0])
+    return jnp.concatenate(rows, axis=0)
+
+
+def update_kernel(sizes, rounds, last, spans, *refs):
+    owners, groups = sum(sizes), len(sizes)
+    codes, values, spends, parts, old, firsts, factors, rest = take(
+        refs, groups, groups, groups, len(spans), rounds - 1, groups, rounds - 1
+    )
+    place = [(g, o) for g, n in enumerate(sizes) for o in range(n)]
+    codes = [codes[g].at[o] for g, o in place]
+    if last:
+        fresh_out, price_out, earned_s, acc, fac, rps, pacc = rest
+    else:
+        fresh_out, price_out, rps_out, earned_s, acc, fac, rps, pacc = rest
+    full = add_prices(list(zip(spans, parts)))
+    now = rounds - 1
+    rps[now] = jnp.where(full > 0.0, 1.0 / full, 1.0)
+    if not last:
+        rps_out[...] = rps[now]
+    for t in range(now):
+        rps[t] = old[t][...]
+    acc[...] = jnp.zeros_like(acc)
+    pacc[...] = jnp.zeros_like(pacc)
+
+    def earn_body(m, carry):
+        for o in range(owners):
+            g, at = place[o]
+            _, k, b = slot_of(codes, o, m)
+            v = values[g][at * HOMES + m].astype(F32)
+            earned = v
+            for t in range(rounds):
+                factor = firsts[g][at * AB_DEV + k] if t == 0 else factors[t - 1][o * AB_DEV + k]
+                earned = v * ((factor * earned) * rps[t, pl.ds(m * IB_DEV + b, 1), :])
+            earned_s[o * HOMES + m] = earned
+            acc[o * AB_DEV + k] += earned
+        return carry
+
+    lax.fori_loop(0, HOMES, earn_body, 0, unroll=UNROLL_E)
+    for r in range(owners * AB_DEV):
+        utility = jnp.sum(acc[r], axis=1, keepdims=True)
+        g, at = place[r // AB_DEV]
+        factor = spends[g][at * AB_DEV + r % AB_DEV] / utility
+        fac[r] = factor
+        if not last:
+            fresh_out[r] = factor
+        elif r < AB_DEV:
+            fresh_out[pl.ds(r, 1), :] = jnp.sum(
+                jnp.where(make_eye(), utility, 0.0), axis=0, keepdims=True
+            )
+
+    def bid_body(m, carry):
+        for o in range(owners):
+            _, k, b = slot_of(codes, o, m)
+            pacc[m * IB_DEV + b] += fold(fac[o * AB_DEV + k] * earned_s[o * HOMES + m])
+        return carry
+
+    lax.fori_loop(0, HOMES, bid_body, 0, unroll=UNROLL_B)
+    for row in range(HOMES * IB_DEV):
+        price_out[pl.ds(row, 1), :] = jnp.sum(pacc[row], axis=0, keepdims=True)
+
+
+UNROLL_V = 16
+WIDE_DOT = False
+JOIN = 2
+UNROLL_B = 8
+UNROLL_E = 2
+
+
+def shaped(shape, dtype=F32):
+    return jax.ShapeDtypeStruct(shape, dtype)
+
+
+PRICE = (HOMES * IB_DEV, BLK)
+PARTIAL = pltpu.VMEM((HOMES * IB_DEV, 8, BLK), F32)
+GRANT = pltpu.CompilerParams(vmem_limit_bytes=LIMIT)
+
+
+def run_values(adv, arrivals, last, *operands):
+    own = arrivals is not None
+    count = len(adv)
+    columns = (count * AB_DEV, BLK, BLK)
+    outs = [
+        shaped((count * HOMES, BLK, BLK), BF16),
+        shaped(columns),
+        shaped(columns),
+        shaped(PRICE),
+        shaped((8, BLK), jnp.int32),
+    ]
+    homes = (HOMES * WIDE, EMB)
+    scratch = [
+        pltpu.SMEM((8, BLK), jnp.int32),
+        pltpu.SemaphoreType.DMA,
+        pltpu.VMEM(columns, F32),
+        PARTIAL,
+    ]
+    if own and last:
+        scratch.insert(0, pltpu.VMEM(homes, BF16))
+    elif own:
+        outs.append(shaped(homes, BF16))
+    return pl.pallas_call(
+        functools.partial(value_kernel, count, arrivals),
+        out_shape=outs,
+        in_specs=[VMEM] * (count + len(operands)),
+        out_specs=[VMEM] * len(outs),
+        scratch_shapes=scratch,
+        compiler_params=GRANT,
+        name="own_values" if own else "more_values",
+    )(*adv, *operands)
+
+
+def run_update(sizes, last, codes, values, spends, spans, parts, old, firsts, factors):
+    owners = sum(sizes)
+    rows = owners * AB_DEV
+    rounds = len(factors) + 1
+    outs = [shaped((AB_DEV, BLK) if last else (rows, BLK, BLK)), shaped(PRICE)]
+    if not last:
+        outs.append(shaped(PRICE))
+    operands = [*values, *spends, *parts, *old, *firsts, *factors]
+    return pl.pallas_call(
+        functools.partial(update_kernel, sizes, rounds, last, spans),
+        out_shape=outs,
+        in_specs=[SMEM] * len(sizes) + [VMEM] * len(operands),
+        out_specs=[VMEM] * len(outs),
+        scratch_shapes=[
+            pltpu.VMEM((owners * HOMES, BLK, BLK), F32),
+            pltpu.VMEM((rows, BLK, BLK), F32),
+            pltpu.VMEM((rows, BLK, BLK), F32),
+            pltpu.VMEM((rounds, *PRICE), F32),
+            PARTIAL,
+        ],
+        compiler_params=GRANT,
+        name="last_update" if last else "update",
+    )(*codes, *operands)
+
+
+def move(x, *masks, cores=(0, 1), flip=0):
+    if len(masks) == 1:
+        masks = masks * 2
+    perm = [
+        (i * 2 + c, (i ^ masks[c]) * 2 + (c ^ flip)) for i in range(HOMES) for c in cores
+    ]
+    return lax.ppermute(x, ("imp", "adv"), perm)
+
+
+def spread(x):
+    held = {0: x}
+    high = [m for m in REP if m != 1]
+    for pick in range(1, 1 << len(high)):
+        d = functools.reduce(lambda a, j: a ^ (high[j] if pick >> j & 1 else 0), range(len(high)), 0)
+        held[d] = move(x, d)
+    if 1 in REP:
+        for d in list(held):
+            held[d ^ 1] = move(held[d], 1)
+    return held
+
+
+def exchange(price, split):
+    for b in split[1:]:
+        shape = (HOMES // (2 * b), 2, b * IB_DEV, BLK)
+        price = price + move(price, b).reshape(shape)[:, ::-1].reshape(PRICE)
+    if not split:
+        return (0, 0), [price, move(price, 0, flip=1)]
+    b = split[0]
+    if JOIN == 0:
+        price = price + move(price, 0, flip=1)
+        return (0, b), [price, move(price, b)]
+    if JOIN == 1:
+        shape = (HOMES // (2 * b), 2, b * IB_DEV, BLK)
+        price = price + move(price, b).reshape(shape)[:, ::-1].reshape(PRICE)
+        return (0, 0), [price, move(price, 0, flip=1)]
+    here = [price, move(price, 0, flip=1)]
+    there = [move(price, b), move(price, b, flip=1)]
+    return (0, 0, b, b), here + there
+
+
+def small_body(imp_emb, adv_emb, allowances, eligible_slots):
+    split = [b for b in (1, 2, 4) if b not in REP]
+    note = jnp.concatenate(
+        [
+            lax.shift_right_logical(allowances, 7).reshape(1, WIDE),
+            lax.bitwise_and(allowances, 127).reshape(1, WIDE),
+            jnp.pad(eligible_slots, ((0, 0), (0, WIDE - HOMES))),
+            jnp.zeros((NOTES - 3, WIDE), jnp.int32),
+        ]
+    )
+    adv = spread(jnp.concatenate([adv_emb, note.astype(BF16)]))
+    near = move(imp_emb, 2, 4)
+    far = move(imp_emb, 6, 1)
+    near_x = move(near, 1)
+    far_x = move(far, 1, cores=(0,))
+    blocks = [
+        near, move(near, 0, flip=1), far, move(far, 0, flip=1), near_x, move(near_x, 0, flip=1)
+    ]
+    tail = move(far_x, 0, cores=(0,), flip=1)
+    arrivals = [(2, 4), (4, 2), (6, 1), (1, 6), (3, 5), (5, 3)]
+    blocks.append(jnp.where(lax.axis_index("adv") == 0, far_x, tail))
+    arrivals.append((7, 7))
+    values, spends, firsts, codes, price, homes = [], [], [], [], None, None
+    for group in GROUPS:
+        first = homes is None
+        v, sp, f, price, c, *rest = run_values(
+            [adv[d] for d in group],
+            tuple(arrivals) if first else None,
+            group is GROUPS[-1],
+            *((imp_emb, *blocks) if first else (homes, price)),
+        )
+        homes = rest[0] if rest else homes
+        values.append(v)
+        spends.append(sp)
+        firsts.append(f)
+        codes.append(c)
+    sizes = tuple(len(group) for group in GROUPS)
+    old, factors = [], []
+    for t in range(ITERS):
+        last = t == ITERS - 1
+        spans, parts = exchange(price, split)
+        fresh, price, *inverse = run_update(
+            sizes, last, codes, values, spends, spans, parts, old, firsts, factors
+        )
+        factors.append(fresh)
+        old.extend(inverse)
+    spans, parts = exchange(price, split)
+    terms = [x[d * IB_DEV : (d + 1) * IB_DEV] for d, x in zip(spans, parts)]
+    while len(terms) > 1:
+        terms = [terms[i] + terms[i + 1] for i in range(0, len(terms), 2)]
+    return terms[0].reshape(IB_DEV * BLK), factors[-1].reshape(AB_DEV * BLK)
+
+
+def small_local(*args):
+    return small_body(*args)
+
+
+def large_local(imp_emb, adv_emb, allowances, eligible_slots):
     slot_count = eligible_slots.shape[1]
     adv_blocks = adv_emb.shape[0] // BLK
     slot_codes = eligible_slots[0]
@@ -82,8 +454,9 @@
 
 
 def solution(mesh):
+    small = mesh.shape["imp"] == HOMES and mesh.shape["adv"] == 2
     return jax.shard_map(
-        local,
+        small_local if small else large_local,
         mesh=mesh,
         in_specs=(
             P(("groups", "imp"), None),

time: 93.4 us -> 47.1 us (0.50)
  blocking collectives: 66.9 us -> 0 us
  starting transfers between devices: 3.62 us -> 22.8 us
  Pallas kernels: 0 us -> 6.97 us
  other arithmetic: 4.45 us -> 1.25 us
  matrix products: 3.02 us -> 0 us
  waiting for transfers between devices: 11.7 us -> 14 us
  local copies, waits for them, and re-layouts: 2.4 us -> 1.09 us
    all_to_all x6 -> x0, blocking collectives: 58.9 us -> none  [the longest x3 27.7 us: local(): lax.all_to_all(totals, 'imp', split_axis=0, concat_axis=0, tiled=True)]
    ppermute x0 -> x20, starting transfers between devices: none -> 22.8 us  [move(): return lax.ppermute(x, ('imp', 'adv'), perm)]
    ppermute x0 -> x20, waiting for transfers between devices: none -> 14 us  [move(): return lax.ppermute(x, ('imp', 'adv'), perm)]
    all_to_all x1 -> x0, waiting for transfers between devices: 11.7 us -> none  [local(): lax.all_to_all(outgoing, 'imp', split_axis=0, concat_axis=0, tiled=True)]
    psum x3 -> x0, blocking collectives: 7.91 us -> none  [local(): home_prices = lax.psum(partial_value, 'adv')]
    pallas_call x0 -> x3, Pallas kernels: none -> 6.97 us  [the longest x2 3.85 us: run_update(): pl.pallas_call(functools.partial(update_kernel, sizes, rounds, last, span...]
    all_to_all x1 -> x0, starting transfers between devices: 3.62 us -> none  [local(): lax.all_to_all(outgoing, 'imp', split_axis=0, concat_axis=0, tiled=True)]
    dot_general x13 -> x0, matrix products: 3.02 us -> none  [the longest x3 0.75 us: local(): jnp.einsum('ok,oj->kj', asked_picker, arrived, precision=highest)]
  transfers between devices with their start and end apart: 1 -> 20, of which waited for: 1 -> 9; matrix products, arithmetic and copies ran while one was open for 1% -> 4% of each run, Pallas kernels for 0% -> 0%
where the time goes in v1:
time: 47.1 us; the launch traced here: 46.9 us
  starting transfers between devices  22.8 us (48%)
  waiting for transfers between devices  14 us (30%)
  Pallas kernels  6.97 us (15%)
  other arithmetic  1.25 us (3%)
  local copies, waits for them, and re-layouts  1.09 us (2%)
  between operations  0.76 us (2%)
    ppermute x20, starting transfers between devices, move(): return lax.ppermute(x, ('imp', 'adv'), perm)  22.8 us
    ppermute x20, waiting for transfers between devices, move(): return lax.ppermute(x, ('imp', 'adv'), perm)  14 us
    pallas_call x2, Pallas kernels, run_update(): pl.pallas_call(functools.partial(update_kernel, sizes, rounds, last, span...  3.85 us
    pallas_call x1, Pallas kernels, run_values(): pl.pallas_call(functools.partial(value_kernel, count, arrivals), out_shap...  3.12 us
    concatenate x1, local copies, waits for them, and re-layouts, small_body(): adv = spread(jnp.concatenate([adv_emb, note.astype(BF16)]))  1.06 us
  transfers between devices with their start and end apart: 20, of which 9 were waited for; matrix products, arithmetic and copies ran while one was open for 4% of the time, Pallas kernels for 0%

profile of v1, /device:TPU:0, one launch (start us, length us, event | category | flops | bytes accessed | tf_op | source)
XLA Modules:
  0.0 46.9 jit_solution(6315372810305731118)
XLA Ops:
  0.6 0.0 copy-start.1
  0.6 5.1 %collective-permute-start.5 = (bf16[256,256]{1,0:T(8,128)(2,1)}, bf16[256,256]{1,0:T(8,128)(2,1)S(1)}, u32[]{:S(2)}, u32[]{:S(2)}) collective-permute-start(bf16[256,256]{1,0:T(8,128)(2,1)} %refs_4_.1), channel_id=1, source_target_pairs={{0,12},{1,3},{2,14},{3,1},{4,8},{5,7},{6,10},{7,5},{8,4},{9,11},{1... | collective-permute-start | bytes 393224 | tf_op jit(solution)/shard_map/ppermute | solution.py:295
  5.8 0.0 collective-permute-start.3
  5.8 0.7 %convert.17 = bf16[1,8]{1,0:T(2,128)(2,1)S(1)} convert(s32[1,8]{1,0:T(1,128)} %param.7) | non-fusion elementwise | flops 8 | bytes 48 | tf_op jit(solution)/shard_map/convert.4
  6.4 3.6 %collective-permute-done.5.refs_7_ = bf16[256,256]{1,0:T(8,128)(2,1)S(1)} collective-permute-done((bf16[256,256]{1,0:T(8,128)(2,1)}, bf16[256,256]{1,0:T(8,128)(2,1)S(1)}, u32[]{:S(2)}, u32[]{:S(2)}) %collective-permute-start.5) | collective-permute-done | bytes 131104 | tf_op jit(solution)/shard_map/ppermute | solution.py:295
  10.0 3.3 %collective-permute-start.9 = (bf16[256,256]{1,0:T(8,128)(2,1)S(1)}, bf16[256,256]{1,0:T(8,128)(2,1)S(1)}, u32[]{:S(2)}, u32[]{:S(2)}) collective-permute-start(bf16[256,256]{1,0:T(8,128)(2,1)S(1)} %collective-permute-done.5.refs_7_), channel_id=1, source_target_pairs={{0,2},{2,0},{4,6},{6,4},{8,10},{10,8},{12,14},{14,12},{16,18},{18,... | collective-permute-start | bytes 393224 | tf_op jit(solution)/shard_map/ppermute | solution.py:295
  13.3 0.0 copy-done.1
  13.4 1.1 %concatenate.6.refs_0_ = bf16[272,256]{1,0:T(8,128)(2,1)S(1)} concatenate(bf16[256,256]{1,0:T(8,128)(2,1)} %param.5, bf16[1,256]{1,0:T(2,128)(2,1)S(1)} %reshape.18, bf16[1,256]{1,0:T(2,128)(2,1)S(1)} %reshape.19, bf16[1,256]{1,0:T(2,128)(2,1)S(1)} %pad.5, bf16[13,256]{1,0:T(8,128)(2,1)S(1)} %broadcast_in_dim.3), dimensions={0} | concatenate | bytes 278528 | tf_op jit(solution)/shard_map/concatenate | solution.py:339
  14.5 2.9 %collective-permute-start.2 = (bf16[272,256]{1,0:T(8,128)(2,1)S(1)}, bf16[272,256]{1,0:T(8,128)(2,1)S(1)}, u32[]{:S(2)}, u32[]{:S(2)}) collective-permute-start(bf16[272,256]{1,0:T(8,128)(2,1)S(1)} %concatenate.6.refs_0_), channel_id=1, source_target_pairs={{0,12},{1,13},{2,14},{3,15},{4,8},{5,9},{6,10},{7,11},{8,4},{9,5},... | collective-permute-start | bytes 417800 | tf_op jit(solution)/shard_map/ppermute | solution.py:295
  17.4 0.0 collective-permute-done.3.refs_5_
  17.4 1.1 %collective-permute-start.7 = (bf16[256,256]{1,0:T(8,128)(2,1)S(1)}, bf16[256,256]{1,0:T(8,128)(2,1)S(1)}, u32[]{:S(2)}, u32[]{:S(2)}) collective-permute-start(bf16[256,256]{1,0:T(8,128)(2,1)S(1)} %collective-permute-done.3.refs_5_), channel_id=1, source_target_pairs={{0,2},{1,3},{2,0},{3,1},{4,6},{5,7},{6,4},{7,5},{8,10},{9,11},{10,... | collective-permute-start | bytes 393224 | tf_op jit(solution)/shard_map/ppermute | solution.py:295
  18.5 0.0 collective-permute-done.9
  18.5 1.3 %collective-permute-start.10 = (bf16[256,256]{1,0:T(8,128)(2,1)S(1)}, bf16[256,256]{1,0:T(8,128)(2,1)S(1)}, u32[]{:S(2)}, u32[]{:S(2)}) collective-permute-start(bf16[256,256]{1,0:T(8,128)(2,1)S(1)} %collective-permute-done.9), channel_id=1, source_target_pairs={{0,1},{2,3},{4,5},{6,7},{8,9},{10,11},{12,13},{14,15},{16,17},{18,... | collective-permute-start | bytes 393224 | tf_op jit(solution)/shard_map/ppermute | solution.py:295
  19.8 2.0 %collective-permute-start.1 = (bf16[272,256]{1,0:T(8,128)(2,1)S(1)}, bf16[272,256]{1,0:T(8,128)(2,1)S(1)}, u32[]{:S(2)}, u32[]{:S(2)}) collective-permute-start(bf16[272,256]{1,0:T(8,128)(2,1)S(1)} %concatenate.6.refs_0_), channel_id=1, source_target_pairs={{0,8},{1,9},{2,10},{3,11},{4,12},{5,13},{6,14},{7,15},{8,0},{9,1},... | collective-permute-start | bytes 417800 | tf_op jit(solution)/shard_map/ppermute | solution.py:295
  21.7 0.5 %collective-permute-start = (bf16[272,256]{1,0:T(8,128)(2,1)S(1)}, bf16[272,256]{1,0:T(8,128)(2,1)S(1)}, u32[]{:S(2)}, u32[]{:S(2)}) collective-permute-start(bf16[272,256]{1,0:T(8,128)(2,1)S(1)} %concatenate.6.refs_0_), channel_id=1, source_target_pairs={{0,4},{1,5},{2,6},{3,7},{4,0},{5,1},{6,2},{7,3},{8,12},{9,13},{10,... | collective-permute-start | bytes 417800 | tf_op jit(solution)/shard_map/ppermute | solution.py:295
  22.2 0.6 %collective-permute-done.2.refs_3_ = bf16[272,256]{1,0:T(8,128)(2,1)S(1)} collective-permute-done((bf16[272,256]{1,0:T(8,128)(2,1)S(1)}, bf16[272,256]{1,0:T(8,128)(2,1)S(1)}, u32[]{:S(2)}, u32[]{:S(2)}) %collective-permute-start.2) | collective-permute-done | bytes 139296 | tf_op jit(solution)/shard_map/ppermute | solution.py:295
  22.8 0.0 collective-permute-start.4
  22.8 0.0 collective-permute-done.7.refs_9_
  22.8 0.5 %collective-permute-start.6 = (bf16[256,256]{1,0:T(8,128)(2,1)S(1)}, bf16[256,256]{1,0:T(8,128)(2,1)S(1)}, u32[]{:S(2)}, u32[]{:S(2)}) collective-permute-start(bf16[256,256]{1,0:T(8,128)(2,1)S(1)} %collective-permute-done.5.refs_7_), channel_id=1, source_target_pairs={{0,1},{1,0},{2,3},{3,2},{4,5},{5,4},{6,7},{7,6},{8,9},{9,8},{10,11... | collective-permute-start | bytes 393224 | tf_op jit(solution)/shard_map/ppermute | solution.py:295
  23.3 0.0 collective-permute-done.10
  23.3 0.1 collective-permute-start.8
  23.4 3.9 %collective-permute-done.1.refs_2_ = bf16[272,256]{1,0:T(8,128)(2,1)S(1)} collective-permute-done((bf16[272,256]{1,0:T(8,128)(2,1)S(1)}, bf16[272,256]{1,0:T(8,128)(2,1)S(1)}, u32[]{:S(2)}, u32[]{:S(2)}) %collective-permute-start.1) | collective-permute-done | bytes 139296 | tf_op jit(solution)/shard_map/ppermute | solution.py:295
  27.3 0.0 collective-permute-done.refs_1_
  27.3 0.0 collective-permute-done.4.refs_6_
  27.3 0.0 collective-permute-done.6.refs_8_
  27.3 0.0 collective-permute-done.8.refs_10_
  27.3 3.1 %own_values.1 = (bf16[32,128,128]{2,1,0:T(8,128)(2,1)S(1)}, f32[8,128,128]{2,1,0:T(8,128)S(1)}, f32[8,128,128]{2,1,0:T(8,128)S(1)}, f32[16,128]{1,0:T(8,128)S(1)}, s32[8,128]{1,0:T(8,128)S(1)}) custom-call(bf16[272,256]{1,0:T(8,128)(2,1)S(1)} %concatenate.6.refs_0_, bf16[272,256]{1,0:T(8,128)(2,1)S(1)} %collective-permute-done.refs_1_, ...), custom_call_target="tpu_custom_call" | custom-call | tf_op jit(solution)/shard_map/own_values/pallas_call | solution.py:253
  30.5 0.1 collective-permute-start.13
  30.5 1.7 %collective-permute-start.12 = (f32[16,128]{1,0:T(8,128)S(1)}, f32[16,128]{1,0:T(8,128)S(1)}, u32[]{:S(2)}, u32[]{:S(2)}) collective-permute-start(f32[16,128]{1,0:T(8,128)S(1)} %get-tuple-element.15.refs_3_), channel_id=1, source_target_pairs={{0,2},{1,3},{2,0},{3,1},{4,6},{5,7},{6,4},{7,5},{8,10},{9,11},{10,... | collective-permute-start | bytes 24584 | tf_op jit(solution)/shard_map/ppermute | solution.py:295
  32.3 0.1 collective-permute-start.11
  32.4 1.2 %collective-permute-done.13.refs_6_ = f32[16,128]{1,0:T(8,128)S(1)} collective-permute-done((f32[16,128]{1,0:T(8,128)S(1)}, f32[16,128]{1,0:T(8,128)S(1)}, u32[]{:S(2)}, u32[]{:S(2)}) %collective-permute-start.13) | collective-permute-done | bytes 8224 | tf_op jit(solution)/shard_map/ppermute | solution.py:295
  33.6 0.7 %collective-permute-done.12.refs_5_ = f32[16,128]{1,0:T(8,128)S(1)} collective-permute-done((f32[16,128]{1,0:T(8,128)S(1)}, f32[16,128]{1,0:T(8,128)S(1)}, u32[]{:S(2)}, u32[]{:S(2)}) %collective-permute-start.12) | collective-permute-done | bytes 8224 | tf_op jit(solution)/shard_map/ppermute | solution.py:295
  34.2 0.0 collective-permute-done.11.refs_4_
  34.3 1.6 %update.1 = (f32[8,128,128]{2,1,0:T(8,128)S(1)}, f32[16,128]{1,0:T(8,128)S(1)}, f32[16,128]{1,0:T(8,128)S(1)}) custom-call(s32[8,128]{1,0:T(8,128)S(1)} %get-tuple-element.12.refs_0_, bf16[32,128,128]{2,1,0:T(8,128)(2,1)S(1)} %get-tuple-element.13.refs_1_, f32[8,128,128]{2,1,0:T(8,128)S(1)} %get-tuple-element.14.refs_2_, ...), custom_call_target="tpu_custom_call" | custom-call | tf_op jit(solution)/shard_map/update/pallas_call | solution.py:272
  35.9 0.8 %collective-permute-start.16 = (f32[16,128]{1,0:T(8,128)S(1)}, f32[16,128]{1,0:T(8,128)S(1)}, u32[]{:S(2)}, u32[]{:S(2)}) collective-permute-start(f32[16,128]{1,0:T(8,128)S(1)} %get-tuple-element.17.refs_3_), channel_id=1, source_target_pairs={{0,3},{1,2},{2,1},{3,0},{4,7},{5,6},{6,5},{7,4},{8,11},{9,10},{10,... | collective-permute-start | bytes 24584 | tf_op jit(solution)/shard_map/ppermute | solution.py:295
  36.7 1.5 %collective-permute-start.15 = (f32[16,128]{1,0:T(8,128)S(1)}, f32[16,128]{1,0:T(8,128)S(1)}, u32[]{:S(2)}, u32[]{:S(2)}) collective-permute-start(f32[16,128]{1,0:T(8,128)S(1)} %get-tuple-element.17.refs_3_), channel_id=1, source_target_pairs={{0,2},{1,3},{2,0},{3,1},{4,6},{5,7},{6,4},{7,5},{8,10},{9,11},{10,... | collective-permute-start | bytes 24584 | tf_op jit(solution)/shard_map/ppermute | solution.py:295
  38.1 0.0 collective-permute-start.14
  38.1 0.9 %collective-permute-done.16.refs_6_ = f32[16,128]{1,0:T(8,128)S(1)} collective-permute-done((f32[16,128]{1,0:T(8,128)S(1)}, f32[16,128]{1,0:T(8,128)S(1)}, u32[]{:S(2)}, u32[]{:S(2)}) %collective-permute-start.16) | collective-permute-done | bytes 8224 | tf_op jit(solution)/shard_map/ppermute | solution.py:295
  39.0 1.3 %collective-permute-done.15.refs_5_ = f32[16,128]{1,0:T(8,128)S(1)} collective-permute-done((f32[16,128]{1,0:T(8,128)S(1)}, f32[16,128]{1,0:T(8,128)S(1)}, u32[]{:S(2)}, u32[]{:S(2)}) %collective-permute-start.15) | collective-permute-done | bytes 8224 | tf_op jit(solution)/shard_map/ppermute | solution.py:295
  40.3 0.0 collective-permute-done.14.refs_4_
  40.3 2.2 %last_update.1 = (f32[2,128]{1,0:T(2,128)}, f32[16,128]{1,0:T(8,128)S(1)}) custom-call(s32[8,128]{1,0:T(8,128)S(1)} %get-tuple-element.12.refs_0_, bf16[32,128,128]{2,1,0:T(8,128)(2,1)S(1)} %get-tuple-element.13.refs_1_, f32[8,128,128]{2,1,0:T(8,128)S(1)} %get-tuple-element.14.refs_2_, f32[16,128]{1,0:T(8,128)S(1)} %get-tuple-element.17.refs_3_, ...), custom_call_target="tpu_custom_call" | custom-call | tf_op jit(solution)/shard_map/last_update/pallas_call | solution.py:272
  42.6 0.1 collective-permute-start.19
  42.6 1.7 %collective-permute-start.18 = (f32[16,128]{1,0:T(8,128)S(1)}, f32[16,128]{1,0:T(8,128)S(1)}, u32[]{:S(2)}, u32[]{:S(2)}) collective-permute-start(f32[16,128]{1,0:T(8,128)S(1)} %get-tuple-element.20), channel_id=1, source_target_pairs={{0,2},{1,3},{2,0},{3,1},{4,6},{5,7},{6,4},{7,5},{8,10},{9,11},{10,... | collective-permute-start | bytes 24584 | tf_op jit(solution)/shard_map/ppermute | solution.py:295
  44.3 0.1 collective-permute-start.17
  44.4 1.2 %collective-permute-done.19 = f32[16,128]{1,0:T(8,128)S(1)} collective-permute-done((f32[16,128]{1,0:T(8,128)S(1)}, f32[16,128]{1,0:T(8,128)S(1)}, u32[]{:S(2)}, u32[]{:S(2)}) %collective-permute-start.19) | collective-permute-done | bytes 8224 | tf_op jit(solution)/shard_map/ppermute | solution.py:295
  45.6 0.6 %collective-permute-done.18 = f32[16,128]{1,0:T(8,128)S(1)} collective-permute-done((f32[16,128]{1,0:T(8,128)S(1)}, f32[16,128]{1,0:T(8,128)S(1)}, u32[]{:S(2)}, u32[]{:S(2)}) %collective-permute-start.18) | collective-permute-done | bytes 8224 | tf_op jit(solution)/shard_map/ppermute | solution.py:295
  46.3 0.0 collective-permute-done.17
  46.3 0.6 %fusion.1 = f32[256]{0:T(256)} fusion(f32[16,128]{1,0:T(8,128)S(1)} %collective-permute-done.19, f32[16,128]{1,0:T(8,128)S(1)} %collective-permute-done.18, f32[16,128]{1,0:T(8,128)S(1)} %collective-permute-done.17, f32[16,128]{1,0:T(8,128)S(1)} %get-tuple-element.20), kind=kLoop, calls=%fused_computation.3 | loop fusion | flops 768 | bytes 5120 | tf_op jit(solution)/shard_map/reshape | solution.py:379
  (8 shorter events, 0.0 us)
Async XLA Ops:
  0.6 12.7 %copy-start.1 = (s32[256]{0:T(256)S(1)}, s32[256]{0:T(256)}, u32[]{:S(2)}) copy-start(s32[256]{0:T(256)} %param.6) | copy-start | bytes 3076
  0.6 9.4 %collective-permute-start.5 = (bf16[256,256]{1,0:T(8,128)(2,1)}, bf16[256,256]{1,0:T(8,128)(2,1)S(1)}, u32[]{:S(2)}, u32[]{:S(2)}) collective-permute-start(bf16[256,256]{1,0:T(8,128)(2,1)} %refs_4_.1), channel_id=1, source_target_pairs={{0,12},{1,3},{2,14},{3,1},{4,8},{5,7},{6,10},{7,5},{8,4},{9,11},{1... | collective-permute-start | bytes 393224 | tf_op jit(solution)/shard_map/ppermute | solution.py:295
  5.8 11.6 %collective-permute-start.3 = (bf16[256,256]{1,0:T(8,128)(2,1)}, bf16[256,256]{1,0:T(8,128)(2,1)S(1)}, u32[]{:S(2)}, u32[]{:S(2)}) collective-permute-start(bf16[256,256]{1,0:T(8,128)(2,1)} %refs_4_.1), channel_id=1, source_target_pairs={{0,4},{1,9},{2,6},{3,11},{4,0},{5,13},{6,2},{7,15},{8,12},{9,1},{1... | collective-permute-start | bytes 393224 | tf_op jit(solution)/shard_map/ppermute | solution.py:295
  10.0 8.4 %collective-permute-start.9 = (bf16[256,256]{1,0:T(8,128)(2,1)S(1)}, bf16[256,256]{1,0:T(8,128)(2,1)S(1)}, u32[]{:S(2)}, u32[]{:S(2)}) collective-permute-start(bf16[256,256]{1,0:T(8,128)(2,1)S(1)} %collective-permute-done.5.refs_7_), channel_id=1, source_target_pairs={{0,2},{2,0},{4,6},{6,4},{8,10},{10,8},{12,14},{14,12},{16,18},{18,... | collective-permute-start | bytes 393224 | tf_op jit(solution)/shard_map/ppermute | solution.py:295
  14.5 8.3 %collective-permute-start.2 = (bf16[272,256]{1,0:T(8,128)(2,1)S(1)}, bf16[272,256]{1,0:T(8,128)(2,1)S(1)}, u32[]{:S(2)}, u32[]{:S(2)}) collective-permute-start(bf16[272,256]{1,0:T(8,128)(2,1)S(1)} %concatenate.6.refs_0_), channel_id=1, source_target_pairs={{0,12},{1,13},{2,14},{3,15},{4,8},{5,9},{6,10},{7,11},{8,4},{9,5},... | collective-permute-start | bytes 417800 | tf_op jit(solution)/shard_map/ppermute | solution.py:295
  17.4 5.4 %collective-permute-start.7 = (bf16[256,256]{1,0:T(8,128)(2,1)S(1)}, bf16[256,256]{1,0:T(8,128)(2,1)S(1)}, u32[]{:S(2)}, u32[]{:S(2)}) collective-permute-start(bf16[256,256]{1,0:T(8,128)(2,1)S(1)} %collective-permute-done.3.refs_5_), channel_id=1, source_target_pairs={{0,2},{1,3},{2,0},{3,1},{4,6},{5,7},{6,4},{7,5},{8,10},{9,11},{10,... | collective-permute-start | bytes 393224 | tf_op jit(solution)/shard_map/ppermute | solution.py:295
  18.5 4.9 %collective-permute-start.10 = (bf16[256,256]{1,0:T(8,128)(2,1)S(1)}, bf16[256,256]{1,0:T(8,128)(2,1)S(1)}, u32[]{:S(2)}, u32[]{:S(2)}) collective-permute-start(bf16[256,256]{1,0:T(8,128)(2,1)S(1)} %collective-permute-done.9), channel_id=1, source_target_pairs={{0,1},{2,3},{4,5},{6,7},{8,9},{10,11},{12,13},{14,15},{16,17},{18,... | collective-permute-start | bytes 393224 | tf_op jit(solution)/shard_map/ppermute | solution.py:295
  19.8 7.5 %collective-permute-start.1 = (bf16[272,256]{1,0:T(8,128)(2,1)S(1)}, bf16[272,256]{1,0:T(8,128)(2,1)S(1)}, u32[]{:S(2)}, u32[]{:S(2)}) collective-permute-start(bf16[272,256]{1,0:T(8,128)(2,1)S(1)} %concatenate.6.refs_0_), channel_id=1, source_target_pairs={{0,8},{1,9},{2,10},{3,11},{4,12},{5,13},{6,14},{7,15},{8,0},{9,1},... | collective-permute-start | bytes 417800 | tf_op jit(solution)/shard_map/ppermute | solution.py:295
  21.7 5.6 %collective-permute-start = (bf16[272,256]{1,0:T(8,128)(2,1)S(1)}, bf16[272,256]{1,0:T(8,128)(2,1)S(1)}, u32[]{:S(2)}, u32[]{:S(2)}) collective-permute-start(bf16[272,256]{1,0:T(8,128)(2,1)S(1)} %concatenate.6.refs_0_), channel_id=1, source_target_pairs={{0,4},{1,5},{2,6},{3,7},{4,0},{5,1},{6,2},{7,3},{8,12},{9,13},{10,... | collective-permute-start | bytes 417800 | tf_op jit(solution)/shard_map/ppermute | solution.py:295
  22.2 5.1 %copy-start = (bf16[256,256]{1,0:T(8,128)(2,1)S(1)}, bf16[256,256]{1,0:T(8,128)(2,1)}, u32[]{:S(2)}) copy-start(bf16[256,256]{1,0:T(8,128)(2,1)} %refs_4_.1) | copy-start | bytes 393220
  22.8 4.5 %collective-permute-start.4 = (bf16[256,256]{1,0:T(8,128)(2,1)S(1)}, bf16[256,256]{1,0:T(8,128)(2,1)S(1)}, u32[]{:S(2)}, u32[]{:S(2)}) collective-permute-start(bf16[256,256]{1,0:T(8,128)(2,1)S(1)} %collective-permute-done.3.refs_5_), channel_id=1, source_target_pairs={{0,1},{1,0},{2,3},{3,2},{4,5},{5,4},{6,7},{7,6},{8,9},{9,8},{10,11... | collective-permute-start | bytes 393224 | tf_op jit(solution)/shard_map/ppermute | solution.py:295
  22.8 4.5 %collective-permute-start.6 = (bf16[256,256]{1,0:T(8,128)(2,1)S(1)}, bf16[256,256]{1,0:T(8,128)(2,1)S(1)}, u32[]{:S(2)}, u32[]{:S(2)}) collective-permute-start(bf16[256,256]{1,0:T(8,128)(2,1)S(1)} %collective-permute-done.5.refs_7_), channel_id=1, source_target_pairs={{0,1},{1,0},{2,3},{3,2},{4,5},{5,4},{6,7},{7,6},{8,9},{9,8},{10,11... | collective-permute-start | bytes 393224 | tf_op jit(solution)/shard_map/ppermute | solution.py:295
  23.3 4.0 %collective-permute-start.8 = (bf16[256,256]{1,0:T(8,128)(2,1)S(1)}, bf16[256,256]{1,0:T(8,128)(2,1)S(1)}, u32[]{:S(2)}, u32[]{:S(2)}) collective-permute-start(bf16[256,256]{1,0:T(8,128)(2,1)S(1)} %collective-permute-done.7.refs_9_), channel_id=1, source_target_pairs={{0,1},{1,0},{2,3},{3,2},{4,5},{5,4},{6,7},{7,6},{8,9},{9,8},{10,11... | collective-permute-start | bytes 393224 | tf_op jit(solution)/shard_map/ppermute | solution.py:295
  30.5 3.1 %collective-permute-start.13 = (f32[16,128]{1,0:T(8,128)S(1)}, f32[16,128]{1,0:T(8,128)S(1)}, u32[]{:S(2)}, u32[]{:S(2)}) collective-permute-start(f32[16,128]{1,0:T(8,128)S(1)} %get-tuple-element.15.refs_3_), channel_id=1, source_target_pairs={{0,3},{1,2},{2,1},{3,0},{4,7},{5,6},{6,5},{7,4},{8,11},{9,10},{10,... | collective-permute-start | bytes 24584 | tf_op jit(solution)/shard_map/ppermute | solution.py:295
  30.5 3.7 %collective-permute-start.12 = (f32[16,128]{1,0:T(8,128)S(1)}, f32[16,128]{1,0:T(8,128)S(1)}, u32[]{:S(2)}, u32[]{:S(2)}) collective-permute-start(f32[16,128]{1,0:T(8,128)S(1)} %get-tuple-element.15.refs_3_), channel_id=1, source_target_pairs={{0,2},{1,3},{2,0},{3,1},{4,6},{5,7},{6,4},{7,5},{8,10},{9,11},{10,... | collective-permute-start | bytes 24584 | tf_op jit(solution)/shard_map/ppermute | solution.py:295
  32.3 2.0 %collective-permute-start.11 = (f32[16,128]{1,0:T(8,128)S(1)}, f32[16,128]{1,0:T(8,128)S(1)}, u32[]{:S(2)}, u32[]{:S(2)}) collective-permute-start(f32[16,128]{1,0:T(8,128)S(1)} %get-tuple-element.15.refs_3_), channel_id=1, source_target_pairs={{0,1},{1,0},{2,3},{3,2},{4,5},{5,4},{6,7},{7,6},{8,9},{9,8},{10,11... | collective-permute-start | bytes 24584 | tf_op jit(solution)/shard_map/ppermute | solution.py:295
  35.9 3.1 %collective-permute-start.16 = (f32[16,128]{1,0:T(8,128)S(1)}, f32[16,128]{1,0:T(8,128)S(1)}, u32[]{:S(2)}, u32[]{:S(2)}) collective-permute-start(f32[16,128]{1,0:T(8,128)S(1)} %get-tuple-element.17.refs_3_), channel_id=1, source_target_pairs={{0,3},{1,2},{2,1},{3,0},{4,7},{5,6},{6,5},{7,4},{8,11},{9,10},{10,... | collective-permute-start | bytes 24584 | tf_op jit(solution)/shard_map/ppermute | solution.py:295
  36.7 3.7 %collective-permute-start.15 = (f32[16,128]{1,0:T(8,128)S(1)}, f32[16,128]{1,0:T(8,128)S(1)}, u32[]{:S(2)}, u32[]{:S(2)}) collective-permute-start(f32[16,128]{1,0:T(8,128)S(1)} %get-tuple-element.17.refs_3_), channel_id=1, source_target_pairs={{0,2},{1,3},{2,0},{3,1},{4,6},{5,7},{6,4},{7,5},{8,10},{9,11},{10,... | collective-permute-start | bytes 24584 | tf_op jit(solution)/shard_map/ppermute | solution.py:295
  38.1 2.2 %collective-permute-start.14 = (f32[16,128]{1,0:T(8,128)S(1)}, f32[16,128]{1,0:T(8,128)S(1)}, u32[]{:S(2)}, u32[]{:S(2)}) collective-permute-start(f32[16,128]{1,0:T(8,128)S(1)} %get-tuple-element.17.refs_3_), channel_id=1, source_target_pairs={{0,1},{1,0},{2,3},{3,2},{4,5},{5,4},{6,7},{7,6},{8,9},{9,8},{10,11... | collective-permute-start | bytes 24584 | tf_op jit(solution)/shard_map/ppermute | solution.py:295
  42.6 3.1 %collective-permute-start.19 = (f32[16,128]{1,0:T(8,128)S(1)}, f32[16,128]{1,0:T(8,128)S(1)}, u32[]{:S(2)}, u32[]{:S(2)}) collective-permute-start(f32[16,128]{1,0:T(8,128)S(1)} %get-tuple-element.20), channel_id=1, source_target_pairs={{0,3},{1,2},{2,1},{3,0},{4,7},{5,6},{6,5},{7,4},{8,11},{9,10},{10,... | collective-permute-start | bytes 24584 | tf_op jit(solution)/shard_map/ppermute | solution.py:295
  42.6 3.7 %collective-permute-start.18 = (f32[16,128]{1,0:T(8,128)S(1)}, f32[16,128]{1,0:T(8,128)S(1)}, u32[]{:S(2)}, u32[]{:S(2)}) collective-permute-start(f32[16,128]{1,0:T(8,128)S(1)} %get-tuple-element.20), channel_id=1, source_target_pairs={{0,2},{1,3},{2,0},{3,1},{4,6},{5,7},{6,4},{7,5},{8,10},{9,11},{10,... | collective-permute-start | bytes 24584 | tf_op jit(solution)/shard_map/ppermute | solution.py:295
  44.3 2.0 %collective-permute-start.17 = (f32[16,128]{1,0:T(8,128)S(1)}, f32[16,128]{1,0:T(8,128)S(1)}, u32[]{:S(2)}, u32[]{:S(2)}) collective-permute-start(f32[16,128]{1,0:T(8,128)S(1)} %get-tuple-element.20), channel_id=1, source_target_pairs={{0,1},{1,0},{2,3},{3,2},{4,5},{5,4},{6,7},{7,6},{8,9},{9,8},{10,11... | collective-permute-start | bytes 24584 | tf_op jit(solution)/shard_map/ppermute | solution.py:295

commit v2 on v1

--- a/solution.py
+++ b/solution.py
@@ -23,7 +23,7 @@
 BF16 = jnp.bfloat16
 SMEM = pl.BlockSpec(memory_space=pltpu.SMEM)
 VMEM = pl.BlockSpec(memory_space=pltpu.VMEM)
-LIMIT = 24 << 20
+LIMIT = 12 << 20
 
 
 def take(refs, *counts):
@@ -42,18 +42,21 @@
 
 def softplus(s):
     e = jnp.exp(-jnp.abs(s))
-    near = e - (e * e) * (0.5 - e * (1.0 / 3.0))
-    return jnp.maximum(s, 0.0) + jnp.where(e < 0.004, near, jnp.log(1.0 + e))
+    near = e - (0.5 * e) * e
+    return jnp.maximum(s, 0.0) + jnp.where(e < 0.001, near, jnp.log(1.0 + e))
 
 
 def fold(tile):
     return jnp.sum(tile.reshape(BLK // 8, 8, BLK), axis=0)
 
 
-def slot_of(codes, owner, home):
-    code = codes[owner][lax.bitwise_xor(lax.axis_index("imp"), home)]
+def slot_of(codes, home, owner, owners):
+    code = codes[lax.bitwise_xor(lax.axis_index("imp"), home)]
     clamped = jnp.maximum(code, 0)
-    return code >= 0, lax.shift_right_logical(clamped, 1), lax.bitwise_and(clamped, 1)
+    k, b = lax.shift_right_logical(clamped, 1), lax.bitwise_and(clamped, 1)
+    live = code >= 0
+    row = jnp.where(live, owner * AB_DEV + k, owners * AB_DEV)
+    return k, b, row, jnp.where(live, home * IB_DEV + b, HOMES * IB_DEV)
 
 
 def row_block(ref, index):
@@ -65,6 +68,31 @@
     for first, second, ref in arrived:
         d = jnp.where(core == 0, first, second)
         imp_s[pl.ds(pl.multiple_of(d * WIDE, WIDE), WIDE), :] = ref[...]
+
+
+def pack_kernel(adv, allow, slots, imp, adv_out, imp_out, allow_s, slots_s, sems):
+    moves = [
+        pltpu.make_async_copy(allow, allow_s, sems.at[0]),
+        pltpu.make_async_copy(slots, slots_s, sems.at[1]),
+        pltpu.make_async_copy(adv, adv_out.at[pl.ds(0, WIDE), :], sems.at[2]),
+        pltpu.make_async_copy(imp, imp_out, sems.at[3]),
+    ]
+    for move in moves:
+        move.start()
+    for move in moves[:2]:
+        move.wait()
+    spend = allow_s[...].reshape(1, WIDE)
+    codes = jnp.concatenate([slots_s[...], jnp.zeros((1, WIDE - HOMES), jnp.int32)], axis=1)
+    rows = [
+        lax.shift_right_logical(spend, 7),
+        lax.bitwise_and(spend, 127),
+        codes,
+        jnp.zeros((NOTES - 3, WIDE), jnp.int32),
+    ]
+    note = jnp.concatenate(rows, axis=0).astype(F32).astype(BF16)
+    adv_out[pl.ds(WIDE, NOTES), :] = note
+    for move in moves[2:]:
+        move.wait()
 
 
 def score(lhs, rhs):
@@ -109,21 +137,12 @@
     acc[...] = jnp.zeros_like(acc)
 
     def value_body(m, carry):
-        slots = [slot_of(codes, o, m) for o in range(count)]
-        picked = [row_block(adv[o], slots[o][1]) for o in range(count)]
-        if WIDE_DOT:
-            rhs = imp_s[pl.ds(pl.multiple_of(m * WIDE, WIDE), WIDE), :]
-            lhs = jnp.concatenate(picked, axis=0)
-            both = score(lhs, rhs)
-        for o, (live, k, b) in enumerate(slots):
-            if WIDE_DOT:
-                s = both[o * BLK : (o + 1) * BLK]
-                s = jnp.where(b == 0, s[:, :BLK], s[:, BLK:])
-            else:
-                s = score(picked[o], row_block(imp_s, m * IB_DEV + b))
-            v = jnp.where(live, softplus(s), 0.0).astype(BF16)
+        for o in range(count):
+            k, b, row, _ = slot_of(codes[o], m, o, count)
+            s = score(row_block(adv[o], k), row_block(imp_s, m * IB_DEV + b))
+            v = softplus(s).astype(BF16).astype(F32)
             values[o * HOMES + m] = v
-            acc[o * AB_DEV + k] += v.astype(F32)
+            acc[row] += v
         return carry
 
     lax.fori_loop(0, HOMES, value_body, 0, unroll=max(1, UNROLL_V // count))
@@ -133,10 +152,8 @@
 
     def bid_body(m, carry):
         for o in range(count):
-            _, k, b = slot_of(codes, o, m)
-            pacc[m * IB_DEV + b] += fold(
-                factor_out[o * AB_DEV + k] * values[o * HOMES + m].astype(F32)
-            )
+            k, _, _, row = slot_of(codes[o], m, o, count)
+            pacc[row] += fold(factor_out[o * AB_DEV + k] * values[o * HOMES + m])
         return carry
 
     lax.fori_loop(0, HOMES, bid_body, 0, unroll=max(1, UNROLL_B // count))
@@ -154,69 +171,58 @@
     return jnp.concatenate(rows, axis=0)
 
 
-def update_kernel(sizes, rounds, last, spans, *refs):
+def update_kernel(sizes, last, spans, *refs):
     owners, groups = sum(sizes), len(sizes)
-    codes, values, spends, parts, old, firsts, factors, rest = take(
-        refs, groups, groups, groups, len(spans), rounds - 1, groups, rounds - 1
-    )
+    codes, values, spends, parts, refs = take(refs, groups, groups, groups, len(spans))
     place = [(g, o) for g, n in enumerate(sizes) for o in range(n)]
     codes = [codes[g].at[o] for g, o in place]
     if last:
-        fresh_out, price_out, earned_s, acc, fac, rps, pacc = rest
+        before, factors, utility_out, price_out, earned_s, acc, fac, rps, pacc = refs
     else:
-        fresh_out, price_out, rps_out, earned_s, acc, fac, rps, pacc = rest
+        firsts, refs = take(refs, groups)
+        fac, price_out, earned_s, acc, rps, pacc = refs
     full = add_prices(list(zip(spans, parts)))
-    now = rounds - 1
-    rps[now] = jnp.where(full > 0.0, 1.0 / full, 1.0)
-    if not last:
-        rps_out[...] = rps[now]
-    for t in range(now):
-        rps[t] = old[t][...]
+    rps[...] = jnp.where(full > 0.0, 1.0 / full, 1.0)
     acc[...] = jnp.zeros_like(acc)
     pacc[...] = jnp.zeros_like(pacc)
 
     def earn_body(m, carry):
-        for o in range(owners):
-            g, at = place[o]
-            _, k, b = slot_of(codes, o, m)
-            v = values[g][at * HOMES + m].astype(F32)
-            earned = v
-            for t in range(rounds):
-                factor = firsts[g][at * AB_DEV + k] if t == 0 else factors[t - 1][o * AB_DEV + k]
-                earned = v * ((factor * earned) * rps[t, pl.ds(m * IB_DEV + b, 1), :])
+        for o, (g, at) in enumerate(place):
+            k, b, row, _ = slot_of(codes[o], m, o, owners)
+            v = values[g][at * HOMES + m]
+            if last:
+                bid = factors[o * AB_DEV + k] * before[o * HOMES + m]
+            else:
+                bid = firsts[g][at * AB_DEV + k] * v
+            earned = v * (bid * rps[pl.ds(m * IB_DEV + b, 1), :])
             earned_s[o * HOMES + m] = earned
-            acc[o * AB_DEV + k] += earned
+            acc[row] += earned
         return carry
 
-    lax.fori_loop(0, HOMES, earn_body, 0, unroll=UNROLL_E)
+    lax.fori_loop(0, HOMES, earn_body, 0, unroll=max(1, UNROLL_E // owners))
     for r in range(owners * AB_DEV):
+        g, at = place[r // AB_DEV]
         utility = jnp.sum(acc[r], axis=1, keepdims=True)
-        g, at = place[r // AB_DEV]
-        factor = spends[g][at * AB_DEV + r % AB_DEV] / utility
-        fac[r] = factor
-        if not last:
-            fresh_out[r] = factor
-        elif r < AB_DEV:
-            fresh_out[pl.ds(r, 1), :] = jnp.sum(
-                jnp.where(make_eye(), utility, 0.0), axis=0, keepdims=True
-            )
+        fac[r] = spends[g][at * AB_DEV + r % AB_DEV] / utility
+        if last and r < AB_DEV:
+            utility_out[r] = fold(jnp.where(make_eye(), utility, 0.0))
 
     def bid_body(m, carry):
         for o in range(owners):
-            _, k, b = slot_of(codes, o, m)
-            pacc[m * IB_DEV + b] += fold(fac[o * AB_DEV + k] * earned_s[o * HOMES + m])
+            k, _, _, row = slot_of(codes[o], m, o, owners)
+            pacc[row] += fold(fac[o * AB_DEV + k] * earned_s[o * HOMES + m])
         return carry
 
-    lax.fori_loop(0, HOMES, bid_body, 0, unroll=UNROLL_B)
+    lax.fori_loop(0, HOMES, bid_body, 0, unroll=max(1, UNROLL_P // owners))
     for row in range(HOMES * IB_DEV):
         price_out[pl.ds(row, 1), :] = jnp.sum(pacc[row], axis=0, keepdims=True)
 
 
+UNROLL_P = 16
 UNROLL_V = 16
-WIDE_DOT = False
 JOIN = 2
-UNROLL_B = 8
-UNROLL_E = 2
+UNROLL_B = 16
+UNROLL_E = 16
 
 
 def shaped(shape, dtype=F32):
@@ -224,8 +230,25 @@
 
 
 PRICE = (HOMES * IB_DEV, BLK)
-PARTIAL = pltpu.VMEM((HOMES * IB_DEV, 8, BLK), F32)
+PARTIAL = pltpu.VMEM((HOMES * IB_DEV + 1, 8, BLK), F32)
 GRANT = pltpu.CompilerParams(vmem_limit_bytes=LIMIT)
+
+
+def run_pack(*operands):
+    operands = [pltpu.with_memory_space_constraint(x, pltpu.HBM) for x in operands]
+    return pl.pallas_call(
+        pack_kernel,
+        out_shape=[shaped((WIDE + NOTES, EMB), BF16), shaped((WIDE, EMB), BF16)],
+        in_specs=[pl.BlockSpec(memory_space=pltpu.HBM)] * 4,
+        out_specs=[VMEM] * 2,
+        scratch_shapes=[
+            pltpu.VMEM((WIDE,), jnp.int32),
+            pltpu.VMEM((1, HOMES), jnp.int32),
+            pltpu.SemaphoreType.DMA((4,)),
+        ],
+        compiler_params=GRANT,
+        name="pack",
+    )(*operands)
 
 
 def run_values(adv, arrivals, last, *operands):
@@ -233,7 +256,7 @@
     count = len(adv)
     columns = (count * AB_DEV, BLK, BLK)
     outs = [
-        shaped((count * HOMES, BLK, BLK), BF16),
+        shaped((count * HOMES, BLK, BLK)),
         shaped(columns),
         shaped(columns),
         shaped(PRICE),
@@ -243,7 +266,7 @@
     scratch = [
         pltpu.SMEM((8, BLK), jnp.int32),
         pltpu.SemaphoreType.DMA,
-        pltpu.VMEM(columns, F32),
+        pltpu.VMEM((count * AB_DEV + 1, BLK, BLK), F32),
         PARTIAL,
     ]
     if own and last:
@@ -257,28 +280,32 @@
         out_specs=[VMEM] * len(outs),
         scratch_shapes=scratch,
         compiler_params=GRANT,
-        name="own_values" if own else "more_values",
     )(*adv, *operands)
 
 
-def run_update(sizes, last, codes, values, spends, spans, parts, old, firsts, factors):
+def run_update(sizes, last, codes, values, spends, spans, parts, before):
     owners = sum(sizes)
     rows = owners * AB_DEV
-    rounds = len(factors) + 1
-    outs = [shaped((AB_DEV, BLK) if last else (rows, BLK, BLK)), shaped(PRICE)]
-    if not last:
-        outs.append(shaped(PRICE))
-    operands = [*values, *spends, *parts, *old, *firsts, *factors]
+    columns = (rows, BLK, BLK)
+    tiles = (owners * HOMES, BLK, BLK)
+    if last:
+        outs = [shaped((AB_DEV, 8, BLK)), shaped(PRICE)]
+        scratch = [pltpu.VMEM(tiles, F32)]
+        extra = [pltpu.VMEM(columns, F32)]
+    else:
+        outs = [shaped(columns), shaped(PRICE), shaped(tiles)]
+        scratch = extra = []
+    operands = [*values, *spends, *parts, *before]
     return pl.pallas_call(
-        functools.partial(update_kernel, sizes, rounds, last, spans),
+        functools.partial(update_kernel, sizes, last, spans),
         out_shape=outs,
         in_specs=[SMEM] * len(sizes) + [VMEM] * len(operands),
         out_specs=[VMEM] * len(outs),
         scratch_shapes=[
-            pltpu.VMEM((owners * HOMES, BLK, BLK), F32),
-            pltpu.VMEM((rows, BLK, BLK), F32),
-            pltpu.VMEM((rows, BLK, BLK), F32),
-            pltpu.VMEM((rounds, *PRICE), F32),
+            *scratch,
+            pltpu.VMEM((rows + 1, BLK, BLK), F32),
+            *extra,
+            pltpu.VMEM(PRICE, F32),
             PARTIAL,
         ],
         compiler_params=GRANT,
@@ -328,15 +355,8 @@
 
 def small_body(imp_emb, adv_emb, allowances, eligible_slots):
     split = [b for b in (1, 2, 4) if b not in REP]
-    note = jnp.concatenate(
-        [
-            lax.shift_right_logical(allowances, 7).reshape(1, WIDE),
-            lax.bitwise_and(allowances, 127).reshape(1, WIDE),
-            jnp.pad(eligible_slots, ((0, 0), (0, WIDE - HOMES))),
-            jnp.zeros((NOTES - 3, WIDE), jnp.int32),
-        ]
-    )
-    adv = spread(jnp.concatenate([adv_emb, note.astype(BF16)]))
+    packed, imp_own = run_pack(adv_emb, allowances, eligible_slots, imp_emb)
+    adv = spread(packed)
     near = move(imp_emb, 2, 4)
     far = move(imp_emb, 6, 1)
     near_x = move(near, 1)
@@ -355,7 +375,7 @@
             [adv[d] for d in group],
             tuple(arrivals) if first else None,
             group is GROUPS[-1],
-            *((imp_emb, *blocks) if first else (homes, price)),
+            *((imp_own, *blocks) if first else (homes, price)),
         )
         homes = rest[0] if rest else homes
         values.append(v)
@@ -363,20 +383,20 @@
         firsts.append(f)
         codes.append(c)
     sizes = tuple(len(group) for group in GROUPS)
-    old, factors = [], []
+    before = firsts
     for t in range(ITERS):
         last = t == ITERS - 1
         spans, parts = exchange(price, split)
-        fresh, price, *inverse = run_update(
-            sizes, last, codes, values, spends, spans, parts, old, firsts, factors
+        fresh, price, *earned = run_update(
+            sizes, last, codes, values, spends, spans, parts, before
         )
-        factors.append(fresh)
-        old.extend(inverse)
+        before = [*earned, fresh]
+    utility = jnp.sum(fresh, axis=1)
     spans, parts = exchange(price, split)
     terms = [x[d * IB_DEV : (d + 1) * IB_DEV] for d, x in zip(spans, parts)]
     while len(terms) > 1:
         terms = [terms[i] + terms[i + 1] for i in range(0, len(terms), 2)]
-    return terms[0].reshape(IB_DEV * BLK), factors[-1].reshape(AB_DEV * BLK)
+    return terms[0].reshape(IB_DEV * BLK), utility.reshape(AB_DEV * BLK)
 
 
 def small_local(*args):

time: 47.1 us -> 46.3 us (0.983)
  local copies, waits for them, and re-layouts: 1.09 us -> 0 us
  starting transfers between devices: 22.8 us -> 23.3 us
    concatenate x1 -> x0, local copies, waits for them, and re-layouts: 1.06 us -> none  [small_body(): adv = spread(jnp.concatenate([adv_emb, note.astype(BF16)]))]
    another operation x2 -> x0, other arithmetic: 0.66 us -> none
    reduce_sum x0 -> x1, other arithmetic: none -> 0.58 us  [small_body(): utility = jnp.sum(fresh, axis=1)]
    ppermute x20, starting transfers between devices: 22.8 us -> 23.3 us  [move(): return lax.ppermute(x, ('imp', 'adv'), perm)]
    pallas_call x2 -> x3, Pallas kernels: 3.85 us -> 4.24 us  [the longest x2 3.2 us: run_update(): pl.pallas_call(functools.partial(update_kernel, sizes, last, spans), out_...]
  transfers between devices with their start and end apart: 20 -> 20, of which waited for: 9 -> 9; matrix products, arithmetic and copies ran while one was open for 4% -> 1% of each run, Pallas kernels for 0% -> 2%
where the time goes in v2:
time: 46.3 us; the launch traced here: 46.1 us
  starting transfers between devices  23.3 us (50%)
  waiting for transfers between devices  13.9 us (30%)
  Pallas kernels  7.13 us (15%)
  other arithmetic  1.16 us (3%)
  between operations  0.71 us (2%)
    ppermute x20, starting transfers between devices, move(): return lax.ppermute(x, ('imp', 'adv'), perm)  23.3 us
    ppermute x20, waiting for transfers between devices, move(): return lax.ppermute(x, ('imp', 'adv'), perm)  13.9 us
    pallas_call x2, Pallas kernels, run_update(): pl.pallas_call(functools.partial(update_kernel, sizes, last, spans), out_...  3.2 us
    pallas_call x1, Pallas kernels, run_values(): pl.pallas_call(functools.partial(value_kernel, count, arrivals), out_shap...  2.89 us
    pallas_call x1, Pallas kernels, run_pack(): pl.pallas_call(pack_kernel, out_shape=[shaped((WIDE + NOTES, EMB), BF16),...  1.03 us
  transfers between devices with their start and end apart: 20, of which 9 were waited for; matrix products, arithmetic and copies ran while one was open for 1% of the time, Pallas kernels for 2%

profile of v2, /device:TPU:0, one launch (start us, length us, event | category | flops | bytes accessed | tf_op | source)
XLA Modules:
  0.0 46.1 jit_solution(13694608761449631194)
XLA Ops:
  0.6 5.1 %collective-permute-start.5 = (bf16[256,256]{1,0:T(8,128)(2,1)}, bf16[256,256]{1,0:T(8,128)(2,1)S(1)}, u32[]{:S(2)}, u32[]{:S(2)}) collective-permute-start(bf16[256,256]{1,0:T(8,128)(2,1)} %imp.1), channel_id=1, source_target_pairs={{0,12},{1,3},{2,14},{3,1},{4,8},{5,7},{6,10},{7,5},{8,4},{9,11},{1... | collective-permute-start | bytes 393224 | tf_op jit(solution)/shard_map/ppermute | solution.py:322
  5.8 0.0 collective-permute-start.3
  5.8 4.2 %collective-permute-done.5.refs_7_ = bf16[256,256]{1,0:T(8,128)(2,1)S(1)} collective-permute-done((bf16[256,256]{1,0:T(8,128)(2,1)}, bf16[256,256]{1,0:T(8,128)(2,1)S(1)}, u32[]{:S(2)}, u32[]{:S(2)}) %collective-permute-start.5) | collective-permute-done | bytes 131104 | tf_op jit(solution)/shard_map/ppermute | solution.py:322
  10.0 3.3 %collective-permute-start.9 = (bf16[256,256]{1,0:T(8,128)(2,1)S(1)}, bf16[256,256]{1,0:T(8,128)(2,1)S(1)}, u32[]{:S(2)}, u32[]{:S(2)}) collective-permute-start(bf16[256,256]{1,0:T(8,128)(2,1)S(1)} %collective-permute-done.5.refs_7_), channel_id=1, source_target_pairs={{0,2},{2,0},{4,6},{6,4},{8,10},{10,8},{12,14},{14,12},{16,18},{18,... | collective-permute-start | bytes 393224 | tf_op jit(solution)/shard_map/ppermute | solution.py:322
  13.3 1.0 %pack.1 = (bf16[272,256]{1,0:T(8,128)(2,1)S(1)}, bf16[256,256]{1,0:T(8,128)(2,1)S(1)}) custom-call(bf16[256,256]{1,0:T(8,128)(2,1)} %adv.1, s32[256]{0:T(256)} %allow.1, s32[1,8]{1,0:T(1,128)} %slots.1, bf16[256,256]{1,0:T(8,128)(2,1)} %imp.1), custom_call_target="tpu_custom_call" | custom-call | tf_op jit(solution)/shard_map/pack/pallas_call | solution.py:239
  14.4 2.9 %collective-permute-start.2 = (bf16[272,256]{1,0:T(8,128)(2,1)S(1)}, bf16[272,256]{1,0:T(8,128)(2,1)S(1)}, u32[]{:S(2)}, u32[]{:S(2)}) collective-permute-start(bf16[272,256]{1,0:T(8,128)(2,1)S(1)} %get-tuple-element.14.refs_0_), channel_id=1, source_target_pairs={{0,12},{1,13},{2,14},{3,15},{4,8},{5,9},{6,10},{7,11},{8,4},{9,5},... | collective-permute-start | bytes 417800 | tf_op jit(solution)/shard_map/ppermute | solution.py:322
  17.3 0.0 collective-permute-done.3.refs_5_
  17.3 1.1 %collective-permute-start.7 = (bf16[256,256]{1,0:T(8,128)(2,1)S(1)}, bf16[256,256]{1,0:T(8,128)(2,1)S(1)}, u32[]{:S(2)}, u32[]{:S(2)}) collective-permute-start(bf16[256,256]{1,0:T(8,128)(2,1)S(1)} %collective-permute-done.3.refs_5_), channel_id=1, source_target_pairs={{0,2},{1,3},{2,0},{3,1},{4,6},{5,7},{6,4},{7,5},{8,10},{9,11},{10,... | collective-permute-start | bytes 393224 | tf_op jit(solution)/shard_map/ppermute | solution.py:322
  18.4 0.0 collective-permute-done.9
  18.4 1.3 %collective-permute-start.10 = (bf16[256,256]{1,0:T(8,128)(2,1)S(1)}, bf16[256,256]{1,0:T(8,128)(2,1)S(1)}, u32[]{:S(2)}, u32[]{:S(2)}) collective-permute-start(bf16[256,256]{1,0:T(8,128)(2,1)S(1)} %collective-permute-done.9), channel_id=1, source_target_pairs={{0,1},{2,3},{4,5},{6,7},{8,9},{10,11},{12,13},{14,15},{16,17},{18,... | collective-permute-start | bytes 393224 | tf_op jit(solution)/shard_map/ppermute | solution.py:322
  19.7 2.1 %collective-permute-start.1 = (bf16[272,256]{1,0:T(8,128)(2,1)S(1)}, bf16[272,256]{1,0:T(8,128)(2,1)S(1)}, u32[]{:S(2)}, u32[]{:S(2)}) collective-permute-start(bf16[272,256]{1,0:T(8,128)(2,1)S(1)} %get-tuple-element.14.refs_0_), channel_id=1, source_target_pairs={{0,8},{1,9},{2,10},{3,11},{4,12},{5,13},{6,14},{7,15},{8,0},{9,1},... | collective-permute-start | bytes 417800 | tf_op jit(solution)/shard_map/ppermute | solution.py:322
  21.7 0.5 %collective-permute-start = (bf16[272,256]{1,0:T(8,128)(2,1)S(1)}, bf16[272,256]{1,0:T(8,128)(2,1)S(1)}, u32[]{:S(2)}, u32[]{:S(2)}) collective-permute-start(bf16[272,256]{1,0:T(8,128)(2,1)S(1)} %get-tuple-element.14.refs_0_), channel_id=1, source_target_pairs={{0,4},{1,5},{2,6},{3,7},{4,0},{5,1},{6,2},{7,3},{8,12},{9,13},{10,... | collective-permute-start | bytes 417800 | tf_op jit(solution)/shard_map/ppermute | solution.py:322
  22.2 0.6 %collective-permute-done.2.refs_3_ = bf16[272,256]{1,0:T(8,128)(2,1)S(1)} collective-permute-done((bf16[272,256]{1,0:T(8,128)(2,1)S(1)}, bf16[272,256]{1,0:T(8,128)(2,1)S(1)}, u32[]{:S(2)}, u32[]{:S(2)}) %collective-permute-start.2) | collective-permute-done | bytes 139296 | tf_op jit(solution)/shard_map/ppermute | solution.py:322
  22.8 0.0 collective-permute-start.6
  22.8 0.0 collective-permute-done.7.refs_9_
  22.8 0.5 %collective-permute-start.4 = (bf16[256,256]{1,0:T(8,128)(2,1)S(1)}, bf16[256,256]{1,0:T(8,128)(2,1)S(1)}, u32[]{:S(2)}, u32[]{:S(2)}) collective-permute-start(bf16[256,256]{1,0:T(8,128)(2,1)S(1)} %collective-permute-done.3.refs_5_), channel_id=1, source_target_pairs={{0,1},{1,0},{2,3},{3,2},{4,5},{5,4},{6,7},{7,6},{8,9},{9,8},{10,11... | collective-permute-start | bytes 393224 | tf_op jit(solution)/shard_map/ppermute | solution.py:322
  23.3 0.0 collective-permute-done.10
  23.3 0.1 collective-permute-start.8
  23.4 3.8 %collective-permute-done.1.refs_2_ = bf16[272,256]{1,0:T(8,128)(2,1)S(1)} collective-permute-done((bf16[272,256]{1,0:T(8,128)(2,1)S(1)}, bf16[272,256]{1,0:T(8,128)(2,1)S(1)}, u32[]{:S(2)}, u32[]{:S(2)}) %collective-permute-start.1) | collective-permute-done | bytes 139296 | tf_op jit(solution)/shard_map/ppermute | solution.py:322
  27.2 0.0 collective-permute-done.refs_1_
  27.2 0.0 collective-permute-done.6.refs_8_
  27.2 0.0 collective-permute-done.4.refs_6_
  27.2 0.0 collective-permute-done.8.refs_10_
  27.2 2.9 %shard_map.59 = (f32[32,128,128]{2,1,0:T(8,128)S(1)}, f32[8,128,128]{2,1,0:T(8,128)S(1)}, f32[8,128,128]{2,1,0:T(8,128)S(1)}, f32[16,128]{1,0:T(8,128)S(1)}, s32[8,128]{1,0:T(8,128)S(1)}) custom-call(bf16[272,256]{1,0:T(8,128)(2,1)S(1)} %get-tuple-element.14.refs_0_, bf16[272,256]{1,0:T(8,128)(2,1)S(1)} %collective-permute-done.refs_1_, ...), custom_call_target="tpu_custom_call" | custom-call | tf_op jit(solution)/shard_map/pallas_call | solution.py:276
  30.1 0.1 collective-permute-start.13
  30.2 1.9 %collective-permute-start.12 = (f32[16,128]{1,0:T(8,128)S(1)}, f32[16,128]{1,0:T(8,128)S(1)}, u32[]{:S(2)}, u32[]{:S(2)}) collective-permute-start(f32[16,128]{1,0:T(8,128)S(1)} %get-tuple-element.19.refs_3_), channel_id=1, source_target_pairs={{0,2},{1,3},{2,0},{3,1},{4,6},{5,7},{6,4},{7,5},{8,10},{9,11},{10,... | collective-permute-start | bytes 24584 | tf_op jit(solution)/shard_map/ppermute | solution.py:322
  32.1 0.0 collective-permute-start.11
  32.2 1.1 %collective-permute-done.13.refs_6_ = f32[16,128]{1,0:T(8,128)S(1)} collective-permute-done((f32[16,128]{1,0:T(8,128)S(1)}, f32[16,128]{1,0:T(8,128)S(1)}, u32[]{:S(2)}, u32[]{:S(2)}) %collective-permute-start.13) | collective-permute-done | bytes 8224 | tf_op jit(solution)/shard_map/ppermute | solution.py:322
  33.2 0.7 %collective-permute-done.12.refs_5_ = f32[16,128]{1,0:T(8,128)S(1)} collective-permute-done((f32[16,128]{1,0:T(8,128)S(1)}, f32[16,128]{1,0:T(8,128)S(1)}, u32[]{:S(2)}, u32[]{:S(2)}) %collective-permute-start.12) | collective-permute-done | bytes 8224 | tf_op jit(solution)/shard_map/ppermute | solution.py:322
  33.9 0.0 collective-permute-done.11.refs_4_
  33.9 1.6 %update.1 = (f32[8,128,128]{2,1,0:T(8,128)S(1)}, f32[16,128]{1,0:T(8,128)S(1)}, f32[32,128,128]{2,1,0:T(8,128)S(1)}) custom-call(s32[8,128]{1,0:T(8,128)S(1)} %get-tuple-element.16.refs_0_, f32[32,128,128]{2,1,0:T(8,128)S(1)} %get-tuple-element.17.refs_1_, f32[8,128,128]{2,1,0:T(8,128)S(1)} %get-tuple-element.18.refs_2_, ...), custom_call_target="tpu_custom_call" | custom-call | tf_op jit(solution)/shard_map/update/pallas_call | solution.py:299
  35.5 1.0 %collective-permute-start.16 = (f32[16,128]{1,0:T(8,128)S(1)}, f32[16,128]{1,0:T(8,128)S(1)}, u32[]{:S(2)}, u32[]{:S(2)}) collective-permute-start(f32[16,128]{1,0:T(8,128)S(1)} %get-tuple-element.21.refs_3_), channel_id=1, source_target_pairs={{0,3},{1,2},{2,1},{3,0},{4,7},{5,6},{6,5},{7,4},{8,11},{9,10},{10,... | collective-permute-start | bytes 24584 | tf_op jit(solution)/shard_map/ppermute | solution.py:322
  36.5 1.4 %collective-permute-start.15 = (f32[16,128]{1,0:T(8,128)S(1)}, f32[16,128]{1,0:T(8,128)S(1)}, u32[]{:S(2)}, u32[]{:S(2)}) collective-permute-start(f32[16,128]{1,0:T(8,128)S(1)} %get-tuple-element.21.refs_3_), channel_id=1, source_target_pairs={{0,2},{1,3},{2,0},{3,1},{4,6},{5,7},{6,4},{7,5},{8,10},{9,11},{10,... | collective-permute-start | bytes 24584 | tf_op jit(solution)/shard_map/ppermute | solution.py:322
  37.9 0.0 collective-permute-start.14
  37.9 0.7 %collective-permute-done.16.refs_6_ = f32[16,128]{1,0:T(8,128)S(1)} collective-permute-done((f32[16,128]{1,0:T(8,128)S(1)}, f32[16,128]{1,0:T(8,128)S(1)}, u32[]{:S(2)}, u32[]{:S(2)}) %collective-permute-start.16) | collective-permute-done | bytes 8224 | tf_op jit(solution)/shard_map/ppermute | solution.py:322
  38.6 1.5 %collective-permute-done.15.refs_5_ = f32[16,128]{1,0:T(8,128)S(1)} collective-permute-done((f32[16,128]{1,0:T(8,128)S(1)}, f32[16,128]{1,0:T(8,128)S(1)}, u32[]{:S(2)}, u32[]{:S(2)}) %collective-permute-start.15) | collective-permute-done | bytes 8224 | tf_op jit(solution)/shard_map/ppermute | solution.py:322
  40.1 0.0 collective-permute-done.14.refs_4_
  40.1 1.6 %last_update.1 = (f32[2,8,128]{2,1,0:T(8,128)S(1)}, f32[16,128]{1,0:T(8,128)S(1)}) custom-call(s32[8,128]{1,0:T(8,128)S(1)} %get-tuple-element.16.refs_0_, f32[32,128,128]{2,1,0:T(8,128)S(1)} %get-tuple-element.17.refs_1_, f32[8,128,128]{2,1,0:T(8,128)S(1)} %get-tuple-element.18.refs_2_, f32[16,128]{1,0:T(8,128)S(1)} %get-tuple-element.21.refs_3_, ...), custom_call_target="tpu_custom_call" | custom-call | tf_op jit(solution)/shard_map/last_update/pallas_call | solution.py:299
  41.8 0.1 collective-permute-start.19
  41.9 1.7 %collective-permute-start.18 = (f32[16,128]{1,0:T(8,128)S(1)}, f32[16,128]{1,0:T(8,128)S(1)}, u32[]{:S(2)}, u32[]{:S(2)}) collective-permute-start(f32[16,128]{1,0:T(8,128)S(1)} %get-tuple-element.24), channel_id=1, source_target_pairs={{0,2},{1,3},{2,0},{3,1},{4,6},{5,7},{6,4},{7,5},{8,10},{9,11},{10,... | collective-permute-start | bytes 24584 | tf_op jit(solution)/shard_map/ppermute | solution.py:322
  43.6 0.1 collective-permute-start.17
  43.7 0.6 %reduce_sum.9 = f32[2,128]{1,0:T(2,128)} reduce(f32[2,8,128]{2,1,0:T(8,128)S(1)} %get-tuple-element.25, f32[]{:T(128)} %constant.2.clone.1), dimensions={1}, to_apply=%region_0.1 | reduce | flops 1792 | bytes 9220 | tf_op jit(solution)/shard_map/reduce_sum | solution.py:394
  44.3 0.6 %collective-permute-done.19 = f32[16,128]{1,0:T(8,128)S(1)} collective-permute-done((f32[16,128]{1,0:T(8,128)S(1)}, f32[16,128]{1,0:T(8,128)S(1)}, u32[]{:S(2)}, u32[]{:S(2)}) %collective-permute-start.19) | collective-permute-done | bytes 8224 | tf_op jit(solution)/shard_map/ppermute | solution.py:322
  44.9 0.7 %collective-permute-done.18 = f32[16,128]{1,0:T(8,128)S(1)} collective-permute-done((f32[16,128]{1,0:T(8,128)S(1)}, f32[16,128]{1,0:T(8,128)S(1)}, u32[]{:S(2)}, u32[]{:S(2)}) %collective-permute-start.18) | collective-permute-done | bytes 8224 | tf_op jit(solution)/shard_map/ppermute | solution.py:322
  45.6 0.0 collective-permute-done.17
  45.6 0.6 %fusion.1 = f32[256]{0:T(256)} fusion(f32[16,128]{1,0:T(8,128)S(1)} %collective-permute-done.19, f32[16,128]{1,0:T(8,128)S(1)} %collective-permute-done.18, f32[16,128]{1,0:T(8,128)S(1)} %collective-permute-done.17, f32[16,128]{1,0:T(8,128)S(1)} %get-tuple-element.24), kind=kLoop, calls=%fused_computation.3 | loop fusion | flops 768 | bytes 5120 | tf_op jit(solution)/shard_map/reshape | solution.py:399
  (1 shorter events, 0.0 us)
Async XLA Ops:
  0.6 9.4 %collective-permute-start.5 = (bf16[256,256]{1,0:T(8,128)(2,1)}, bf16[256,256]{1,0:T(8,128)(2,1)S(1)}, u32[]{:S(2)}, u32[]{:S(2)}) collective-permute-start(bf16[256,256]{1,0:T(8,128)(2,1)} %imp.1), channel_id=1, source_target_pairs={{0,12},{1,3},{2,14},{3,1},{4,8},{5,7},{6,10},{7,5},{8,4},{9,11},{1... | collective-permute-start | bytes 393224 | tf_op jit(solution)/shard_map/ppermute | solution.py:322
  5.8 11.5 %collective-permute-start.3 = (bf16[256,256]{1,0:T(8,128)(2,1)}, bf16[256,256]{1,0:T(8,128)(2,1)S(1)}, u32[]{:S(2)}, u32[]{:S(2)}) collective-permute-start(bf16[256,256]{1,0:T(8,128)(2,1)} %imp.1), channel_id=1, source_target_pairs={{0,4},{1,9},{2,6},{3,11},{4,0},{5,13},{6,2},{7,15},{8,12},{9,1},{1... | collective-permute-start | bytes 393224 | tf_op jit(solution)/shard_map/ppermute | solution.py:322
  10.0 8.4 %collective-permute-start.9 = (bf16[256,256]{1,0:T(8,128)(2,1)S(1)}, bf16[256,256]{1,0:T(8,128)(2,1)S(1)}, u32[]{:S(2)}, u32[]{:S(2)}) collective-permute-start(bf16[256,256]{1,0:T(8,128)(2,1)S(1)} %collective-permute-done.5.refs_7_), channel_id=1, source_target_pairs={{0,2},{2,0},{4,6},{6,4},{8,10},{10,8},{12,14},{14,12},{16,18},{18,... | collective-permute-start | bytes 393224 | tf_op jit(solution)/shard_map/ppermute | solution.py:322
  14.4 8.4 %collective-permute-start.2 = (bf16[272,256]{1,0:T(8,128)(2,1)S(1)}, bf16[272,256]{1,0:T(8,128)(2,1)S(1)}, u32[]{:S(2)}, u32[]{:S(2)}) collective-permute-start(bf16[272,256]{1,0:T(8,128)(2,1)S(1)} %get-tuple-element.14.refs_0_), channel_id=1, source_target_pairs={{0,12},{1,13},{2,14},{3,15},{4,8},{5,9},{6,10},{7,11},{8,4},{9,5},... | collective-permute-start | bytes 417800 | tf_op jit(solution)/shard_map/ppermute | solution.py:322
  17.3 5.5 %collective-permute-start.7 = (bf16[256,256]{1,0:T(8,128)(2,1)S(1)}, bf16[256,256]{1,0:T(8,128)(2,1)S(1)}, u32[]{:S(2)}, u32[]{:S(2)}) collective-permute-start(bf16[256,256]{1,0:T(8,128)(2,1)S(1)} %collective-permute-done.3.refs_5_), channel_id=1, source_target_pairs={{0,2},{1,3},{2,0},{3,1},{4,6},{5,7},{6,4},{7,5},{8,10},{9,11},{10,... | collective-permute-start | bytes 393224 | tf_op jit(solution)/shard_map/ppermute | solution.py:322
  18.4 4.9 %collective-permute-start.10 = (bf16[256,256]{1,0:T(8,128)(2,1)S(1)}, bf16[256,256]{1,0:T(8,128)(2,1)S(1)}, u32[]{:S(2)}, u32[]{:S(2)}) collective-permute-start(bf16[256,256]{1,0:T(8,128)(2,1)S(1)} %collective-permute-done.9), channel_id=1, source_target_pairs={{0,1},{2,3},{4,5},{6,7},{8,9},{10,11},{12,13},{14,15},{16,17},{18,... | collective-permute-start | bytes 393224 | tf_op jit(solution)/shard_map/ppermute | solution.py:322
  19.7 7.5 %collective-permute-start.1 = (bf16[272,256]{1,0:T(8,128)(2,1)S(1)}, bf16[272,256]{1,0:T(8,128)(2,1)S(1)}, u32[]{:S(2)}, u32[]{:S(2)}) collective-permute-start(bf16[272,256]{1,0:T(8,128)(2,1)S(1)} %get-tuple-element.14.refs_0_), channel_id=1, source_target_pairs={{0,8},{1,9},{2,10},{3,11},{4,12},{5,13},{6,14},{7,15},{8,0},{9,1},... | collective-permute-start | bytes 417800 | tf_op jit(solution)/shard_map/ppermute | solution.py:322
  21.7 5.5 %collective-permute-start = (bf16[272,256]{1,0:T(8,128)(2,1)S(1)}, bf16[272,256]{1,0:T(8,128)(2,1)S(1)}, u32[]{:S(2)}, u32[]{:S(2)}) collective-permute-start(bf16[272,256]{1,0:T(8,128)(2,1)S(1)} %get-tuple-element.14.refs_0_), channel_id=1, source_target_pairs={{0,4},{1,5},{2,6},{3,7},{4,0},{5,1},{6,2},{7,3},{8,12},{9,13},{10,... | collective-permute-start | bytes 417800 | tf_op jit(solution)/shard_map/ppermute | solution.py:322
  22.8 4.4 %collective-permute-start.6 = (bf16[256,256]{1,0:T(8,128)(2,1)S(1)}, bf16[256,256]{1,0:T(8,128)(2,1)S(1)}, u32[]{:S(2)}, u32[]{:S(2)}) collective-permute-start(bf16[256,256]{1,0:T(8,128)(2,1)S(1)} %collective-permute-done.5.refs_7_), channel_id=1, source_target_pairs={{0,1},{1,0},{2,3},{3,2},{4,5},{5,4},{6,7},{7,6},{8,9},{9,8},{10,11... | collective-permute-start | bytes 393224 | tf_op jit(solution)/shard_map/ppermute | solution.py:322
  22.8 4.4 %collective-permute-start.4 = (bf16[256,256]{1,0:T(8,128)(2,1)S(1)}, bf16[256,256]{1,0:T(8,128)(2,1)S(1)}, u32[]{:S(2)}, u32[]{:S(2)}) collective-permute-start(bf16[256,256]{1,0:T(8,128)(2,1)S(1)} %collective-permute-done.3.refs_5_), channel_id=1, source_target_pairs={{0,1},{1,0},{2,3},{3,2},{4,5},{5,4},{6,7},{7,6},{8,9},{9,8},{10,11... | collective-permute-start | bytes 393224 | tf_op jit(solution)/shard_map/ppermute | solution.py:322
  23.3 3.9 %collective-permute-start.8 = (bf16[256,256]{1,0:T(8,128)(2,1)S(1)}, bf16[256,256]{1,0:T(8,128)(2,1)S(1)}, u32[]{:S(2)}, u32[]{:S(2)}) collective-permute-start(bf16[256,256]{1,0:T(8,128)(2,1)S(1)} %collective-permute-done.7.refs_9_), channel_id=1, source_target_pairs={{0,1},{1,0},{2,3},{3,2},{4,5},{5,4},{6,7},{7,6},{8,9},{9,8},{10,11... | collective-permute-start | bytes 393224 | tf_op jit(solution)/shard_map/ppermute | solution.py:322
  30.1 3.1 %collective-permute-start.13 = (f32[16,128]{1,0:T(8,128)S(1)}, f32[16,128]{1,0:T(8,128)S(1)}, u32[]{:S(2)}, u32[]{:S(2)}) collective-permute-start(f32[16,128]{1,0:T(8,128)S(1)} %get-tuple-element.19.refs_3_), channel_id=1, source_target_pairs={{0,3},{1,2},{2,1},{3,0},{4,7},{5,6},{6,5},{7,4},{8,11},{9,10},{10,... | collective-permute-start | bytes 24584 | tf_op jit(solution)/shard_map/ppermute | solution.py:322
  30.2 3.7 %collective-permute-start.12 = (f32[16,128]{1,0:T(8,128)S(1)}, f32[16,128]{1,0:T(8,128)S(1)}, u32[]{:S(2)}, u32[]{:S(2)}) collective-permute-start(f32[16,128]{1,0:T(8,128)S(1)} %get-tuple-element.19.refs_3_), channel_id=1, source_target_pairs={{0,2},{1,3},{2,0},{3,1},{4,6},{5,7},{6,4},{7,5},{8,10},{9,11},{10,... | collective-permute-start | bytes 24584 | tf_op jit(solution)/shard_map/ppermute | solution.py:322
  32.1 1.8 %collective-permute-start.11 = (f32[16,128]{1,0:T(8,128)S(1)}, f32[16,128]{1,0:T(8,128)S(1)}, u32[]{:S(2)}, u32[]{:S(2)}) collective-permute-start(f32[16,128]{1,0:T(8,128)S(1)} %get-tuple-element.19.refs_3_), channel_id=1, source_target_pairs={{0,1},{1,0},{2,3},{3,2},{4,5},{5,4},{6,7},{7,6},{8,9},{9,8},{10,11... | collective-permute-start | bytes 24584 | tf_op jit(solution)/shard_map/ppermute | solution.py:322
  35.5 3.1 %collective-permute-start.16 = (f32[16,128]{1,0:T(8,128)S(1)}, f32[16,128]{1,0:T(8,128)S(1)}, u32[]{:S(2)}, u32[]{:S(2)}) collective-permute-start(f32[16,128]{1,0:T(8,128)S(1)} %get-tuple-element.21.refs_3_), channel_id=1, source_target_pairs={{0,3},{1,2},{2,1},{3,0},{4,7},{5,6},{6,5},{7,4},{8,11},{9,10},{10,... | collective-permute-start | bytes 24584 | tf_op jit(solution)/shard_map/ppermute | solution.py:322
  36.5 3.7 %collective-permute-start.15 = (f32[16,128]{1,0:T(8,128)S(1)}, f32[16,128]{1,0:T(8,128)S(1)}, u32[]{:S(2)}, u32[]{:S(2)}) collective-permute-start(f32[16,128]{1,0:T(8,128)S(1)} %get-tuple-element.21.refs_3_), channel_id=1, source_target_pairs={{0,2},{1,3},{2,0},{3,1},{4,6},{5,7},{6,4},{7,5},{8,10},{9,11},{10,... | collective-permute-start | bytes 24584 | tf_op jit(solution)/shard_map/ppermute | solution.py:322
  37.9 2.2 %collective-permute-start.14 = (f32[16,128]{1,0:T(8,128)S(1)}, f32[16,128]{1,0:T(8,128)S(1)}, u32[]{:S(2)}, u32[]{:S(2)}) collective-permute-start(f32[16,128]{1,0:T(8,128)S(1)} %get-tuple-element.21.refs_3_), channel_id=1, source_target_pairs={{0,1},{1,0},{2,3},{3,2},{4,5},{5,4},{6,7},{7,6},{8,9},{9,8},{10,11... | collective-permute-start | bytes 24584 | tf_op jit(solution)/shard_map/ppermute | solution.py:322
  41.8 3.1 %collective-permute-start.19 = (f32[16,128]{1,0:T(8,128)S(1)}, f32[16,128]{1,0:T(8,128)S(1)}, u32[]{:S(2)}, u32[]{:S(2)}) collective-permute-start(f32[16,128]{1,0:T(8,128)S(1)} %get-tuple-element.24), channel_id=1, source_target_pairs={{0,3},{1,2},{2,1},{3,0},{4,7},{5,6},{6,5},{7,4},{8,11},{9,10},{10,... | collective-permute-start | bytes 24584 | tf_op jit(solution)/shard_map/ppermute | solution.py:322
  41.9 3.7 %collective-permute-start.18 = (f32[16,128]{1,0:T(8,128)S(1)}, f32[16,128]{1,0:T(8,128)S(1)}, u32[]{:S(2)}, u32[]{:S(2)}) collective-permute-start(f32[16,128]{1,0:T(8,128)S(1)} %get-tuple-element.24), channel_id=1, source_target_pairs={{0,2},{1,3},{2,0},{3,1},{4,6},{5,7},{6,4},{7,5},{8,10},{9,11},{10,... | collective-permute-start | bytes 24584 | tf_op jit(solution)/shard_map/ppermute | solution.py:322
  43.6 2.0 %collective-permute-start.17 = (f32[16,128]{1,0:T(8,128)S(1)}, f32[16,128]{1,0:T(8,128)S(1)}, u32[]{:S(2)}, u32[]{:S(2)}) collective-permute-start(f32[16,128]{1,0:T(8,128)S(1)} %get-tuple-element.24), channel_id=1, source_target_pairs={{0,1},{1,0},{2,3},{3,2},{4,5},{5,4},{6,7},{7,6},{8,9},{9,8},{10,11... | collective-permute-start | bytes 24584 | tf_op jit(solution)/shard_map/ppermute | solution.py:322

commit v3 on v2

--- a/solution.py
+++ b/solution.py
@@ -40,8 +40,13 @@
     )
 
 
-def softplus(s):
-    e = jnp.exp(-jnp.abs(s))
+def softplus(dot):
+    scale = 1.0 / math.sqrt(EMB)
+    s = dot * scale
+    if FOLDED:
+        e = jnp.exp2(jnp.abs(dot) * (-scale / math.log(2.0)))
+    else:
+        e = jnp.exp(-jnp.abs(s))
     near = e - (0.5 * e) * e
     return jnp.maximum(s, 0.0) + jnp.where(e < 0.001, near, jnp.log(1.0 + e))
 
@@ -96,9 +101,7 @@
 
 
 def score(lhs, rhs):
-    return lax.dot_general(
-        lhs, rhs, (((1,), (1,)), ((), ())), preferred_element_type=F32
-    ) * (1.0 / math.sqrt(EMB))
+    return lax.dot_general(lhs, rhs, (((1,), (1,)), ((), ())), preferred_element_type=F32)
 
 
 def value_kernel(count, arrivals, *refs):
@@ -171,7 +174,7 @@
     return jnp.concatenate(rows, axis=0)
 
 
-def update_kernel(sizes, last, spans, *refs):
+def update_kernel(sizes, last, spans, wanted, *refs):
     owners, groups = sum(sizes), len(sizes)
     codes, values, spends, parts, refs = take(refs, groups, groups, groups, len(spans))
     place = [(g, o) for g, n in enumerate(sizes) for o in range(n)]
@@ -213,16 +216,28 @@
             pacc[row] += fold(fac[o * AB_DEV + k] * earned_s[o * HOMES + m])
         return carry
 
-    lax.fori_loop(0, HOMES, bid_body, 0, unroll=max(1, UNROLL_P // owners))
-    for row in range(HOMES * IB_DEV):
-        price_out[pl.ds(row, 1), :] = jnp.sum(pacc[row], axis=0, keepdims=True)
-
-
-UNROLL_P = 16
-UNROLL_V = 16
+    if last:
+        for m in wanted:
+            bid_body(m, 0)
+    else:
+        lax.fori_loop(0, HOMES, bid_body, 0, unroll=max(1, UNROLL_P // owners))
+    for at, m in enumerate(wanted):
+        for b in range(IB_DEV):
+            total = jnp.sum(pacc[m * IB_DEV + b], axis=0, keepdims=True)
+            if last:
+                price_out[at, pl.ds(b, 1), :] = total
+            else:
+                price_out[pl.ds(m * IB_DEV + b, 1), :] = total
+
+
+UNROLL_P = 32
+UNROLL_V = 32
 JOIN = 2
-UNROLL_B = 16
-UNROLL_E = 16
+NEAR, FAR = (2, 4), (6, 1)
+FOLDED = True
+DIRECT = False
+UNROLL_B = 32
+UNROLL_E = 32
 
 
 def shaped(shape, dtype=F32):
@@ -283,13 +298,13 @@
     )(*adv, *operands)
 
 
-def run_update(sizes, last, codes, values, spends, spans, parts, before):
+def run_update(sizes, last, codes, values, spends, spans, parts, wanted, before):
     owners = sum(sizes)
     rows = owners * AB_DEV
     columns = (rows, BLK, BLK)
     tiles = (owners * HOMES, BLK, BLK)
     if last:
-        outs = [shaped((AB_DEV, 8, BLK)), shaped(PRICE)]
+        outs = [shaped((AB_DEV, 8, BLK)), shaped((len(wanted), IB_DEV, BLK))]
         scratch = [pltpu.VMEM(tiles, F32)]
         extra = [pltpu.VMEM(columns, F32)]
     else:
@@ -297,7 +312,7 @@
         scratch = extra = []
     operands = [*values, *spends, *parts, *before]
     return pl.pallas_call(
-        functools.partial(update_kernel, sizes, last, spans),
+        functools.partial(update_kernel, sizes, last, spans, wanted),
         out_shape=outs,
         in_specs=[SMEM] * len(sizes) + [VMEM] * len(operands),
         out_specs=[VMEM] * len(outs),
@@ -357,17 +372,21 @@
     split = [b for b in (1, 2, 4) if b not in REP]
     packed, imp_own = run_pack(adv_emb, allowances, eligible_slots, imp_emb)
     adv = spread(packed)
-    near = move(imp_emb, 2, 4)
-    far = move(imp_emb, 6, 1)
+    near = move(imp_emb, *NEAR)
+    far = move(imp_emb, *FAR)
     near_x = move(near, 1)
     far_x = move(far, 1, cores=(0,))
     blocks = [
         near, move(near, 0, flip=1), far, move(far, 0, flip=1), near_x, move(near_x, 0, flip=1)
     ]
-    tail = move(far_x, 0, cores=(0,), flip=1)
-    arrivals = [(2, 4), (4, 2), (6, 1), (1, 6), (3, 5), (5, 3)]
+    if DIRECT:
+        tail = move(far, 1, cores=(0,), flip=1)
+    else:
+        tail = move(far_x, 0, cores=(0,), flip=1)
+    arrivals = [NEAR, NEAR[::-1], FAR, FAR[::-1]]
+    arrivals += [tuple(d ^ 1 for d in pair) for pair in arrivals[:2]]
     blocks.append(jnp.where(lax.axis_index("adv") == 0, far_x, tail))
-    arrivals.append((7, 7))
+    arrivals.append((FAR[0] ^ 1, FAR[0] ^ 1))
     values, spends, firsts, codes, price, homes = [], [], [], [], None, None
     for group in GROUPS:
         first = homes is None
@@ -387,13 +406,18 @@
     for t in range(ITERS):
         last = t == ITERS - 1
         spans, parts = exchange(price, split)
+        wanted = (0, *split) if last else tuple(range(HOMES))
         fresh, price, *earned = run_update(
-            sizes, last, codes, values, spends, spans, parts, before
+            sizes, last, codes, values, spends, spans, parts, wanted, before
         )
         before = [*earned, fresh]
     utility = jnp.sum(fresh, axis=1)
-    spans, parts = exchange(price, split)
-    terms = [x[d * IB_DEV : (d + 1) * IB_DEV] for d, x in zip(spans, parts)]
+    here = price[0]
+    terms = [here, move(here, 0, flip=1)]
+    for at, b in enumerate(split, 1):
+        there = price[at]
+        terms.append(move(there, b))
+        terms.append(move(there, b, flip=1))
     while len(terms) > 1:
         terms = [terms[i] + terms[i + 1] for i in range(0, len(terms), 2)]
     return terms[0].reshape(IB_DEV * BLK), utility.reshape(AB_DEV * BLK)

time: 46.3 us -> 47.2 us (1.019)
  waiting for transfers between devices: 13.9 us -> 15 us
  Pallas kernels: 7.13 us -> 6.57 us
    ppermute x20, waiting for transfers between devices: 13.9 us -> 15 us  [move(): return lax.ppermute(x, ('imp', 'adv'), perm)]
where the time goes in v3:
time: 47.2 us; the launch traced here: 47 us
  starting transfers between devices  23.5 us (50%)
  waiting for transfers between devices  15 us (32%)
  Pallas kernels  6.57 us (14%)
  other arithmetic  1.16 us (2%)
  between operations  0.71 us (2%)
    ppermute x20, starting transfers between devices, move(): return lax.ppermute(x, ('imp', 'adv'), perm)  23.5 us
    ppermute x20, waiting for transfers between devices, move(): return lax.ppermute(x, ('imp', 'adv'), perm)  15 us
    pallas_call x2, Pallas kernels, run_update(): pl.pallas_call(functools.partial(update_kernel, sizes, last, spans, wante...  2.93 us
    pallas_call x1, Pallas kernels, run_values(): pl.pallas_call(functools.partial(value_kernel, count, arrivals), out_shap...  2.61 us
    pallas_call x1, Pallas kernels, run_pack(): pl.pallas_call(pack_kernel, out_shape=[shaped((WIDE + NOTES, EMB), BF16),...  1.03 us
  transfers between devices with their start and end apart: 20, of which 9 were waited for; matrix products, arithmetic and copies ran while one was open for 1% of the time, Pallas kernels for 2%

profile of v3, /device:TPU:0, one launch (start us, length us, event | category | flops | bytes accessed | tf_op | source)
XLA Modules:
  0.0 47.0 jit_solution(14310411403537411359)
XLA Ops:
  0.6 5.1 %collective-permute-start.5 = (bf16[256,256]{1,0:T(8,128)(2,1)}, bf16[256,256]{1,0:T(8,128)(2,1)S(1)}, u32[]{:S(2)}, u32[]{:S(2)}) collective-permute-start(bf16[256,256]{1,0:T(8,128)(2,1)} %imp.1), channel_id=1, source_target_pairs={{0,12},{1,3},{2,14},{3,1},{4,8},{5,7},{6,10},{7,5},{8,4},{9,11},{1... | collective-permute-start | bytes 393224 | tf_op jit(solution)/shard_map/ppermute | solution.py:337
  5.8 0.0 collective-permute-start.3
  5.8 4.2 %collective-permute-done.5.refs_7_ = bf16[256,256]{1,0:T(8,128)(2,1)S(1)} collective-permute-done((bf16[256,256]{1,0:T(8,128)(2,1)}, bf16[256,256]{1,0:T(8,128)(2,1)S(1)}, u32[]{:S(2)}, u32[]{:S(2)}) %collective-permute-start.5) | collective-permute-done | bytes 131104 | tf_op jit(solution)/shard_map/ppermute | solution.py:337
  10.0 3.3 %collective-permute-start.9 = (bf16[256,256]{1,0:T(8,128)(2,1)S(1)}, bf16[256,256]{1,0:T(8,128)(2,1)S(1)}, u32[]{:S(2)}, u32[]{:S(2)}) collective-permute-start(bf16[256,256]{1,0:T(8,128)(2,1)S(1)} %collective-permute-done.5.refs_7_), channel_id=1, source_target_pairs={{0,2},{2,0},{4,6},{6,4},{8,10},{10,8},{12,14},{14,12},{16,18},{18,... | collective-permute-start | bytes 393224 | tf_op jit(solution)/shard_map/ppermute | solution.py:337
  13.3 1.0 %pack.1 = (bf16[272,256]{1,0:T(8,128)(2,1)S(1)}, bf16[256,256]{1,0:T(8,128)(2,1)S(1)}) custom-call(bf16[256,256]{1,0:T(8,128)(2,1)} %adv.1, s32[256]{0:T(256)} %allow.1, s32[1,8]{1,0:T(1,128)} %slots.1, bf16[256,256]{1,0:T(8,128)(2,1)} %imp.1), custom_call_target="tpu_custom_call" | custom-call | tf_op jit(solution)/shard_map/pack/pallas_call | solution.py:254
  14.4 2.9 %collective-permute-start.2 = (bf16[272,256]{1,0:T(8,128)(2,1)S(1)}, bf16[272,256]{1,0:T(8,128)(2,1)S(1)}, u32[]{:S(2)}, u32[]{:S(2)}) collective-permute-start(bf16[272,256]{1,0:T(8,128)(2,1)S(1)} %get-tuple-element.14.refs_0_), channel_id=1, source_target_pairs={{0,12},{1,13},{2,14},{3,15},{4,8},{5,9},{6,10},{7,11},{8,4},{9,5},... | collective-permute-start | bytes 417800 | tf_op jit(solution)/shard_map/ppermute | solution.py:337
  17.3 0.0 collective-permute-done.3.refs_5_
  17.3 1.1 %collective-permute-start.7 = (bf16[256,256]{1,0:T(8,128)(2,1)S(1)}, bf16[256,256]{1,0:T(8,128)(2,1)S(1)}, u32[]{:S(2)}, u32[]{:S(2)}) collective-permute-start(bf16[256,256]{1,0:T(8,128)(2,1)S(1)} %collective-permute-done.3.refs_5_), channel_id=1, source_target_pairs={{0,2},{1,3},{2,0},{3,1},{4,6},{5,7},{6,4},{7,5},{8,10},{9,11},{10,... | collective-permute-start | bytes 393224 | tf_op jit(solution)/shard_map/ppermute | solution.py:337
  18.4 0.0 collective-permute-done.9
  18.4 1.3 %collective-permute-start.10 = (bf16[256,256]{1,0:T(8,128)(2,1)S(1)}, bf16[256,256]{1,0:T(8,128)(2,1)S(1)}, u32[]{:S(2)}, u32[]{:S(2)}) collective-permute-start(bf16[256,256]{1,0:T(8,128)(2,1)S(1)} %collective-permute-done.9), channel_id=1, source_target_pairs={{0,1},{2,3},{4,5},{6,7},{8,9},{10,11},{12,13},{14,15},{16,17},{18,... | collective-permute-start | bytes 393224 | tf_op jit(solution)/shard_map/ppermute | solution.py:337
  19.7 2.1 %collective-permute-start.1 = (bf16[272,256]{1,0:T(8,128)(2,1)S(1)}, bf16[272,256]{1,0:T(8,128)(2,1)S(1)}, u32[]{:S(2)}, u32[]{:S(2)}) collective-permute-start(bf16[272,256]{1,0:T(8,128)(2,1)S(1)} %get-tuple-element.14.refs_0_), channel_id=1, source_target_pairs={{0,8},{1,9},{2,10},{3,11},{4,12},{5,13},{6,14},{7,15},{8,0},{9,1},... | collective-permute-start | bytes 417800 | tf_op jit(solution)/shard_map/ppermute | solution.py:337
  21.7 0.5 %collective-permute-start = (bf16[272,256]{1,0:T(8,128)(2,1)S(1)}, bf16[272,256]{1,0:T(8,128)(2,1)S(1)}, u32[]{:S(2)}, u32[]{:S(2)}) collective-permute-start(bf16[272,256]{1,0:T(8,128)(2,1)S(1)} %get-tuple-element.14.refs_0_), channel_id=1, source_target_pairs={{0,4},{1,5},{2,6},{3,7},{4,0},{5,1},{6,2},{7,3},{8,12},{9,13},{10,... | collective-permute-start | bytes 417800 | tf_op jit(solution)/shard_map/ppermute | solution.py:337
  22.2 0.6 %collective-permute-done.2.refs_3_ = bf16[272,256]{1,0:T(8,128)(2,1)S(1)} collective-permute-done((bf16[272,256]{1,0:T(8,128)(2,1)S(1)}, bf16[272,256]{1,0:T(8,128)(2,1)S(1)}, u32[]{:S(2)}, u32[]{:S(2)}) %collective-permute-start.2) | collective-permute-done | bytes 139296 | tf_op jit(solution)/shard_map/ppermute | solution.py:337
  22.8 0.0 collective-permute-start.6
  22.8 0.0 collective-permute-done.7.refs_9_
  22.8 0.5 %collective-permute-start.4 = (bf16[256,256]{1,0:T(8,128)(2,1)S(1)}, bf16[256,256]{1,0:T(8,128)(2,1)S(1)}, u32[]{:S(2)}, u32[]{:S(2)}) collective-permute-start(bf16[256,256]{1,0:T(8,128)(2,1)S(1)} %collective-permute-done.3.refs_5_), channel_id=1, source_target_pairs={{0,1},{1,0},{2,3},{3,2},{4,5},{5,4},{6,7},{7,6},{8,9},{9,8},{10,11... | collective-permute-start | bytes 393224 | tf_op jit(solution)/shard_map/ppermute | solution.py:337
  23.3 0.0 collective-permute-done.10
  23.3 0.1 collective-permute-start.8
  23.4 3.8 %collective-permute-done.1.refs_2_ = bf16[272,256]{1,0:T(8,128)(2,1)S(1)} collective-permute-done((bf16[272,256]{1,0:T(8,128)(2,1)S(1)}, bf16[272,256]{1,0:T(8,128)(2,1)S(1)}, u32[]{:S(2)}, u32[]{:S(2)}) %collective-permute-start.1) | collective-permute-done | bytes 139296 | tf_op jit(solution)/shard_map/ppermute | solution.py:337
  27.2 0.0 collective-permute-done.refs_1_
  27.2 0.0 collective-permute-done.6.refs_8_
  27.2 0.0 collective-permute-done.4.refs_6_
  27.2 0.0 collective-permute-done.8.refs_10_
  27.2 2.6 %shard_map.59 = (f32[32,128,128]{2,1,0:T(8,128)S(1)}, f32[8,128,128]{2,1,0:T(8,128)S(1)}, f32[8,128,128]{2,1,0:T(8,128)S(1)}, f32[16,128]{1,0:T(8,128)S(1)}, s32[8,128]{1,0:T(8,128)S(1)}) custom-call(bf16[272,256]{1,0:T(8,128)(2,1)S(1)} %get-tuple-element.14.refs_0_, bf16[272,256]{1,0:T(8,128)(2,1)S(1)} %collective-permute-done.refs_1_, ...), custom_call_target="tpu_custom_call" | custom-call | tf_op jit(solution)/shard_map/pallas_call | solution.py:291
  29.8 0.1 collective-permute-start.13
  29.9 1.9 %collective-permute-start.12 = (f32[16,128]{1,0:T(8,128)S(1)}, f32[16,128]{1,0:T(8,128)S(1)}, u32[]{:S(2)}, u32[]{:S(2)}) collective-permute-start(f32[16,128]{1,0:T(8,128)S(1)} %get-tuple-element.19.refs_3_), channel_id=1, source_target_pairs={{0,2},{1,3},{2,0},{3,1},{4,6},{5,7},{6,4},{7,5},{8,10},{9,11},{10,... | collective-permute-start | bytes 24584 | tf_op jit(solution)/shard_map/ppermute | solution.py:337
  31.8 0.0 collective-permute-start.11
  31.9 1.1 %collective-permute-done.13.refs_6_ = f32[16,128]{1,0:T(8,128)S(1)} collective-permute-done((f32[16,128]{1,0:T(8,128)S(1)}, f32[16,128]{1,0:T(8,128)S(1)}, u32[]{:S(2)}, u32[]{:S(2)}) %collective-permute-start.13) | collective-permute-done | bytes 8224 | tf_op jit(solution)/shard_map/ppermute | solution.py:337
  33.0 0.7 %collective-permute-done.12.refs_5_ = f32[16,128]{1,0:T(8,128)S(1)} collective-permute-done((f32[16,128]{1,0:T(8,128)S(1)}, f32[16,128]{1,0:T(8,128)S(1)}, u32[]{:S(2)}, u32[]{:S(2)}) %collective-permute-start.12) | collective-permute-done | bytes 8224 | tf_op jit(solution)/shard_map/ppermute | solution.py:337
  33.6 0.0 collective-permute-done.11.refs_4_
  33.6 1.5 %update.1 = (f32[8,128,128]{2,1,0:T(8,128)S(1)}, f32[16,128]{1,0:T(8,128)S(1)}, f32[32,128,128]{2,1,0:T(8,128)S(1)}) custom-call(s32[8,128]{1,0:T(8,128)S(1)} %get-tuple-element.16.refs_0_, f32[32,128,128]{2,1,0:T(8,128)S(1)} %get-tuple-element.17.refs_1_, f32[8,128,128]{2,1,0:T(8,128)S(1)} %get-tuple-element.18.refs_2_, ...), custom_call_target="tpu_custom_call" | custom-call | tf_op jit(solution)/shard_map/update/pallas_call | solution.py:314
  35.2 1.0 %collective-permute-start.16 = (f32[16,128]{1,0:T(8,128)S(1)}, f32[16,128]{1,0:T(8,128)S(1)}, u32[]{:S(2)}, u32[]{:S(2)}) collective-permute-start(f32[16,128]{1,0:T(8,128)S(1)} %get-tuple-element.21.refs_3_), channel_id=1, source_target_pairs={{0,3},{1,2},{2,1},{3,0},{4,7},{5,6},{6,5},{7,4},{8,11},{9,10},{10,... | collective-permute-start | bytes 24584 | tf_op jit(solution)/shard_map/ppermute | solution.py:337
  36.1 1.5 %collective-permute-start.15 = (f32[16,128]{1,0:T(8,128)S(1)}, f32[16,128]{1,0:T(8,128)S(1)}, u32[]{:S(2)}, u32[]{:S(2)}) collective-permute-start(f32[16,128]{1,0:T(8,128)S(1)} %get-tuple-element.21.refs_3_), channel_id=1, source_target_pairs={{0,2},{1,3},{2,0},{3,1},{4,6},{5,7},{6,4},{7,5},{8,10},{9,11},{10,... | collective-permute-start | bytes 24584 | tf_op jit(solution)/shard_map/ppermute | solution.py:337
  37.6 0.0 collective-permute-start.14
  37.6 0.7 %collective-permute-done.16.refs_6_ = f32[16,128]{1,0:T(8,128)S(1)} collective-permute-done((f32[16,128]{1,0:T(8,128)S(1)}, f32[16,128]{1,0:T(8,128)S(1)}, u32[]{:S(2)}, u32[]{:S(2)}) %collective-permute-start.16) | collective-permute-done | bytes 8224 | tf_op jit(solution)/shard_map/ppermute | solution.py:337
  38.3 1.5 %collective-permute-done.15.refs_5_ = f32[16,128]{1,0:T(8,128)S(1)} collective-permute-done((f32[16,128]{1,0:T(8,128)S(1)}, f32[16,128]{1,0:T(8,128)S(1)}, u32[]{:S(2)}, u32[]{:S(2)}) %collective-permute-start.15) | collective-permute-done | bytes 8224 | tf_op jit(solution)/shard_map/ppermute | solution.py:337
  39.8 0.0 collective-permute-done.14.refs_4_
  39.8 1.4 %last_update.1 = (f32[2,8,128]{2,1,0:T(8,128)S(1)}, f32[2,2,128]{2,1,0:T(2,128)S(1)}) custom-call(s32[8,128]{1,0:T(8,128)S(1)} %get-tuple-element.16.refs_0_, f32[32,128,128]{2,1,0:T(8,128)S(1)} %get-tuple-element.17.refs_1_, f32[8,128,128]{2,1,0:T(8,128)S(1)} %get-tuple-element.18.refs_2_, f32[16,128]{1,0:T(8,128)S(1)} %get-tuple-element.21.refs_3_, ...), custom_call_target="tpu_custom_call" | custom-call | tf_op jit(solution)/shard_map/last_update/pallas_call | solution.py:314
  41.2 0.2 collective-permute-start.17
  41.4 1.4 %collective-permute-start.19 = (f32[2,128]{1,0:T(2,128)S(1)}, f32[2,128]{1,0:T(2,128)S(1)}, u32[]{:S(2)}, u32[]{:S(2)}) collective-permute-start(f32[2,128]{1,0:T(2,128)S(1)} %get-tuple-element.27), channel_id=1, source_target_pairs={{0,3},{1,2},{2,1},{3,0},{4,7},{5,6},{6,5},{7,4},{8,11},{9,10},{10,... | collective-permute-start | bytes 3080 | tf_op jit(solution)/shard_map/ppermute | solution.py:337
  42.8 0.6 %collective-permute-start.18 = (f32[2,128]{1,0:T(2,128)S(1)}, f32[2,128]{1,0:T(2,128)S(1)}, u32[]{:S(2)}, u32[]{:S(2)}) collective-permute-start(f32[2,128]{1,0:T(2,128)S(1)} %get-tuple-element.27), channel_id=1, source_target_pairs={{0,2},{1,3},{2,0},{3,1},{4,6},{5,7},{6,4},{7,5},{8,10},{9,11},{10,... | collective-permute-start | bytes 3080 | tf_op jit(solution)/shard_map/ppermute | solution.py:337
  43.4 0.6 %reduce_sum.9 = f32[2,128]{1,0:T(2,128)} reduce(f32[2,8,128]{2,1,0:T(8,128)S(1)} %get-tuple-element.25, f32[]{:T(128)} %constant.2.clone.1), dimensions={1}, to_apply=%region_0.1 | reduce | flops 1792 | bytes 9220 | tf_op jit(solution)/shard_map/reduce_sum | solution.py:414
  44.0 0.0 collective-permute-done.17
  44.0 0.4 collective-permute-done.19
  44.4 2.0 %collective-permute-done.18 = f32[2,128]{1,0:T(2,128)S(1)} collective-permute-done((f32[2,128]{1,0:T(2,128)S(1)}, f32[2,128]{1,0:T(2,128)S(1)}, u32[]{:S(2)}, u32[]{:S(2)}) %collective-permute-start.18) | collective-permute-done | bytes 1056 | tf_op jit(solution)/shard_map/ppermute | solution.py:337
  46.4 0.6 %add_bitcast_fusion = f32[256]{0:T(256)} fusion(f32[2,128]{1,0:T(2,128)S(1)} %collective-permute-done.18, f32[2,128]{1,0:T(2,128)S(1)} %collective-permute-done.19, f32[2,128]{1,0:T(2,128)S(1)} %collective-permute-done.17, f32[2,2,128]{2,1,0:T(2,128)S(1)} %get-tuple-element.24), kind=kLoop, calls=%fused_computation.1 | loop fusion | flops 768 | bytes 5120 | tf_op jit(solution)/shard_map/reshape | solution.py:423
  (2 shorter events, 0.0 us)
Async XLA Ops:
  0.6 9.4 %collective-permute-start.5 = (bf16[256,256]{1,0:T(8,128)(2,1)}, bf16[256,256]{1,0:T(8,128)(2,1)S(1)}, u32[]{:S(2)}, u32[]{:S(2)}) collective-permute-start(bf16[256,256]{1,0:T(8,128)(2,1)} %imp.1), channel_id=1, source_target_pairs={{0,12},{1,3},{2,14},{3,1},{4,8},{5,7},{6,10},{7,5},{8,4},{9,11},{1... | collective-permute-start | bytes 393224 | tf_op jit(solution)/shard_map/ppermute | solution.py:337
  5.8 11.5 %collective-permute-start.3 = (bf16[256,256]{1,0:T(8,128)(2,1)}, bf16[256,256]{1,0:T(8,128)(2,1)S(1)}, u32[]{:S(2)}, u32[]{:S(2)}) collective-permute-start(bf16[256,256]{1,0:T(8,128)(2,1)} %imp.1), channel_id=1, source_target_pairs={{0,4},{1,9},{2,6},{3,11},{4,0},{5,13},{6,2},{7,15},{8,12},{9,1},{1... | collective-permute-start | bytes 393224 | tf_op jit(solution)/shard_map/ppermute | solution.py:337
  10.0 8.4 %collective-permute-start.9 = (bf16[256,256]{1,0:T(8,128)(2,1)S(1)}, bf16[256,256]{1,0:T(8,128)(2,1)S(1)}, u32[]{:S(2)}, u32[]{:S(2)}) collective-permute-start(bf16[256,256]{1,0:T(8,128)(2,1)S(1)} %collective-permute-done.5.refs_7_), channel_id=1, source_target_pairs={{0,2},{2,0},{4,6},{6,4},{8,10},{10,8},{12,14},{14,12},{16,18},{18,... | collective-permute-start | bytes 393224 | tf_op jit(solution)/shard_map/ppermute | solution.py:337
  14.4 8.4 %collective-permute-start.2 = (bf16[272,256]{1,0:T(8,128)(2,1)S(1)}, bf16[272,256]{1,0:T(8,128)(2,1)S(1)}, u32[]{:S(2)}, u32[]{:S(2)}) collective-permute-start(bf16[272,256]{1,0:T(8,128)(2,1)S(1)} %get-tuple-element.14.refs_0_), channel_id=1, source_target_pairs={{0,12},{1,13},{2,14},{3,15},{4,8},{5,9},{6,10},{7,11},{8,4},{9,5},... | collective-permute-start | bytes 417800 | tf_op jit(solution)/shard_map/ppermute | solution.py:337
  17.3 5.5 %collective-permute-start.7 = (bf16[256,256]{1,0:T(8,128)(2,1)S(1)}, bf16[256,256]{1,0:T(8,128)(2,1)S(1)}, u32[]{:S(2)}, u32[]{:S(2)}) collective-permute-start(bf16[256,256]{1,0:T(8,128)(2,1)S(1)} %collective-permute-done.3.refs_5_), channel_id=1, source_target_pairs={{0,2},{1,3},{2,0},{3,1},{4,6},{5,7},{6,4},{7,5},{8,10},{9,11},{10,... | collective-permute-start | bytes 393224 | tf_op jit(solution)/shard_map/ppermute | solution.py:337
  18.4 4.9 %collective-permute-start.10 = (bf16[256,256]{1,0:T(8,128)(2,1)S(1)}, bf16[256,256]{1,0:T(8,128)(2,1)S(1)}, u32[]{:S(2)}, u32[]{:S(2)}) collective-permute-start(bf16[256,256]{1,0:T(8,128)(2,1)S(1)} %collective-permute-done.9), channel_id=1, source_target_pairs={{0,1},{2,3},{4,5},{6,7},{8,9},{10,11},{12,13},{14,15},{16,17},{18,... | collective-permute-start | bytes 393224 | tf_op jit(solution)/shard_map/ppermute | solution.py:337
  19.7 7.5 %collective-permute-start.1 = (bf16[272,256]{1,0:T(8,128)(2,1)S(1)}, bf16[272,256]{1,0:T(8,128)(2,1)S(1)}, u32[]{:S(2)}, u32[]{:S(2)}) collective-permute-start(bf16[272,256]{1,0:T(8,128)(2,1)S(1)} %get-tuple-element.14.refs_0_), channel_id=1, source_target_pairs={{0,8},{1,9},{2,10},{3,11},{4,12},{5,13},{6,14},{7,15},{8,0},{9,1},... | collective-permute-start | bytes 417800 | tf_op jit(solution)/shard_map/ppermute | solution.py:337
  21.7 5.5 %collective-permute-start = (bf16[272,256]{1,0:T(8,128)(2,1)S(1)}, bf16[272,256]{1,0:T(8,128)(2,1)S(1)}, u32[]{:S(2)}, u32[]{:S(2)}) collective-permute-start(bf16[272,256]{1,0:T(8,128)(2,1)S(1)} %get-tuple-element.14.refs_0_), channel_id=1, source_target_pairs={{0,4},{1,5},{2,6},{3,7},{4,0},{5,1},{6,2},{7,3},{8,12},{9,13},{10,... | collective-permute-start | bytes 417800 | tf_op jit(solution)/shard_map/ppermute | solution.py:337
  22.8 4.4 %collective-permute-start.6 = (bf16[256,256]{1,0:T(8,128)(2,1)S(1)}, bf16[256,256]{1,0:T(8,128)(2,1)S(1)}, u32[]{:S(2)}, u32[]{:S(2)}) collective-permute-start(bf16[256,256]{1,0:T(8,128)(2,1)S(1)} %collective-permute-done.5.refs_7_), channel_id=1, source_target_pairs={{0,1},{1,0},{2,3},{3,2},{4,5},{5,4},{6,7},{7,6},{8,9},{9,8},{10,11... | collective-permute-start | bytes 393224 | tf_op jit(solution)/shard_map/ppermute | solution.py:337
  22.8 4.4 %collective-permute-start.4 = (bf16[256,256]{1,0:T(8,128)(2,1)S(1)}, bf16[256,256]{1,0:T(8,128)(2,1)S(1)}, u32[]{:S(2)}, u32[]{:S(2)}) collective-permute-start(bf16[256,256]{1,0:T(8,128)(2,1)S(1)} %collective-permute-done.3.refs_5_), channel_id=1, source_target_pairs={{0,1},{1,0},{2,3},{3,2},{4,5},{5,4},{6,7},{7,6},{8,9},{9,8},{10,11... | collective-permute-start | bytes 393224 | tf_op jit(solution)/shard_map/ppermute | solution.py:337
  23.3 3.9 %collective-permute-start.8 = (bf16[256,256]{1,0:T(8,128)(2,1)S(1)}, bf16[256,256]{1,0:T(8,128)(2,1)S(1)}, u32[]{:S(2)}, u32[]{:S(2)}) collective-permute-start(bf16[256,256]{1,0:T(8,128)(2,1)S(1)} %collective-permute-done.7.refs_9_), channel_id=1, source_target_pairs={{0,1},{1,0},{2,3},{3,2},{4,5},{5,4},{6,7},{7,6},{8,9},{9,8},{10,11... | collective-permute-start | bytes 393224 | tf_op jit(solution)/shard_map/ppermute | solution.py:337
  29.8 3.1 %collective-permute-start.13 = (f32[16,128]{1,0:T(8,128)S(1)}, f32[16,128]{1,0:T(8,128)S(1)}, u32[]{:S(2)}, u32[]{:S(2)}) collective-permute-start(f32[16,128]{1,0:T(8,128)S(1)} %get-tuple-element.19.refs_3_), channel_id=1, source_target_pairs={{0,3},{1,2},{2,1},{3,0},{4,7},{5,6},{6,5},{7,4},{8,11},{9,10},{10,... | collective-permute-start | bytes 24584 | tf_op jit(solution)/shard_map/ppermute | solution.py:337
  29.9 3.7 %collective-permute-start.12 = (f32[16,128]{1,0:T(8,128)S(1)}, f32[16,128]{1,0:T(8,128)S(1)}, u32[]{:S(2)}, u32[]{:S(2)}) collective-permute-start(f32[16,128]{1,0:T(8,128)S(1)} %get-tuple-element.19.refs_3_), channel_id=1, source_target_pairs={{0,2},{1,3},{2,0},{3,1},{4,6},{5,7},{6,4},{7,5},{8,10},{9,11},{10,... | collective-permute-start | bytes 24584 | tf_op jit(solution)/shard_map/ppermute | solution.py:337
  31.8 1.8 %collective-permute-start.11 = (f32[16,128]{1,0:T(8,128)S(1)}, f32[16,128]{1,0:T(8,128)S(1)}, u32[]{:S(2)}, u32[]{:S(2)}) collective-permute-start(f32[16,128]{1,0:T(8,128)S(1)} %get-tuple-element.19.refs_3_), channel_id=1, source_target_pairs={{0,1},{1,0},{2,3},{3,2},{4,5},{5,4},{6,7},{7,6},{8,9},{9,8},{10,11... | collective-permute-start | bytes 24584 | tf_op jit(solution)/shard_map/ppermute | solution.py:337
  35.2 3.1 %collective-permute-start.16 = (f32[16,128]{1,0:T(8,128)S(1)}, f32[16,128]{1,0:T(8,128)S(1)}, u32[]{:S(2)}, u32[]{:S(2)}) collective-permute-start(f32[16,128]{1,0:T(8,128)S(1)} %get-tuple-element.21.refs_3_), channel_id=1, source_target_pairs={{0,3},{1,2},{2,1},{3,0},{4,7},{5,6},{6,5},{7,4},{8,11},{9,10},{10,... | collective-permute-start | bytes 24584 | tf_op jit(solution)/shard_map/ppermute | solution.py:337
  36.1 3.7 %collective-permute-start.15 = (f32[16,128]{1,0:T(8,128)S(1)}, f32[16,128]{1,0:T(8,128)S(1)}, u32[]{:S(2)}, u32[]{:S(2)}) collective-permute-start(f32[16,128]{1,0:T(8,128)S(1)} %get-tuple-element.21.refs_3_), channel_id=1, source_target_pairs={{0,2},{1,3},{2,0},{3,1},{4,6},{5,7},{6,4},{7,5},{8,10},{9,11},{10,... | collective-permute-start | bytes 24584 | tf_op jit(solution)/shard_map/ppermute | solution.py:337
  37.6 2.2 %collective-permute-start.14 = (f32[16,128]{1,0:T(8,128)S(1)}, f32[16,128]{1,0:T(8,128)S(1)}, u32[]{:S(2)}, u32[]{:S(2)}) collective-permute-start(f32[16,128]{1,0:T(8,128)S(1)} %get-tuple-element.21.refs_3_), channel_id=1, source_target_pairs={{0,1},{1,0},{2,3},{3,2},{4,5},{5,4},{6,7},{7,6},{8,9},{9,8},{10,11... | collective-permute-start | bytes 24584 | tf_op jit(solution)/shard_map/ppermute | solution.py:337
  41.2 2.8 %collective-permute-start.17 = (f32[2,128]{1,0:T(2,128)S(1)}, f32[2,128]{1,0:T(2,128)S(1)}, u32[]{:S(2)}, u32[]{:S(2)}) collective-permute-start(f32[2,128]{1,0:T(2,128)S(1)} %get-tuple-element.26), channel_id=1, source_target_pairs={{0,1},{1,0},{2,3},{3,2},{4,5},{5,4},{6,7},{7,6},{8,9},{9,8},{10,11... | collective-permute-start | bytes 3080 | tf_op jit(solution)/shard_map/ppermute | solution.py:337
  41.4 3.0 %collective-permute-start.19 = (f32[2,128]{1,0:T(2,128)S(1)}, f32[2,128]{1,0:T(2,128)S(1)}, u32[]{:S(2)}, u32[]{:S(2)}) collective-permute-start(f32[2,128]{1,0:T(2,128)S(1)} %get-tuple-element.27), channel_id=1, source_target_pairs={{0,3},{1,2},{2,1},{3,0},{4,7},{5,6},{6,5},{7,4},{8,11},{9,10},{10,... | collective-permute-start | bytes 3080 | tf_op jit(solution)/shard_map/ppermute | solution.py:337
  42.8 3.6 %collective-permute-start.18 = (f32[2,128]{1,0:T(2,128)S(1)}, f32[2,128]{1,0:T(2,128)S(1)}, u32[]{:S(2)}, u32[]{:S(2)}) collective-permute-start(f32[2,128]{1,0:T(2,128)S(1)} %get-tuple-element.27), channel_id=1, source_target_pairs={{0,2},{1,3},{2,0},{3,1},{4,6},{5,7},{6,4},{7,5},{8,10},{9,11},{10,... | collective-permute-start | bytes 3080 | tf_op jit(solution)/shard_map/ppermute | solution.py:337

commit v4 on v3

--- a/solution.py
+++ b/solution.py
@@ -178,7 +178,13 @@
     owners, groups = sum(sizes), len(sizes)
     codes, values, spends, parts, refs = take(refs, groups, groups, groups, len(spans))
     place = [(g, o) for g, n in enumerate(sizes) for o in range(n)]
-    codes = [codes[g].at[o] for g, o in place]
+    refs, (tables, sems) = refs[:-2], refs[-2:]
+    copies = [
+        pltpu.make_async_copy(codes[g], tables.at[g], sems.at[g]) for g in range(groups)
+    ]
+    for copy in copies:
+        copy.start()
+    codes = [tables.at[g, o] for g, o in place]
     if last:
         before, factors, utility_out, price_out, earned_s, acc, fac, rps, pacc = refs
     else:
@@ -188,6 +194,8 @@
     rps[...] = jnp.where(full > 0.0, 1.0 / full, 1.0)
     acc[...] = jnp.zeros_like(acc)
     pacc[...] = jnp.zeros_like(pacc)
+    for copy in copies:
+        copy.wait()
 
     def earn_body(m, carry):
         for o, (g, at) in enumerate(place):
@@ -314,7 +322,7 @@
     return pl.pallas_call(
         functools.partial(update_kernel, sizes, last, spans, wanted),
         out_shape=outs,
-        in_specs=[SMEM] * len(sizes) + [VMEM] * len(operands),
+        in_specs=[VMEM] * (len(sizes) + len(operands)),
         out_specs=[VMEM] * len(outs),
         scratch_shapes=[
             *scratch,
@@ -322,6 +330,8 @@
             *extra,
             pltpu.VMEM(PRICE, F32),
             PARTIAL,
+            pltpu.SMEM((len(sizes), 8, BLK), jnp.int32),
+            pltpu.SemaphoreType.DMA((len(sizes),)),
         ],
         compiler_params=GRANT,
         name="last_update" if last else "update",

time: 47.2 us -> 47.1 us (level)
  no operation moved by 1% of the time
where the time goes in v4:
time: 47.1 us; the launch traced here: 46.9 us
  starting transfers between devices  23.5 us (50%)
  waiting for transfers between devices  15 us (32%)
  Pallas kernels  6.52 us (14%)
  other arithmetic  1.16 us (2%)
  between operations  0.73 us (2%)
    ppermute x20, starting transfers between devices, move(): return lax.ppermute(x, ('imp', 'adv'), perm)  23.5 us
    ppermute x20, waiting for transfers between devices, move(): return lax.ppermute(x, ('imp', 'adv'), perm)  15 us
    pallas_call x2, Pallas kernels, run_update(): pl.pallas_call(functools.partial(update_kernel, sizes, last, spans, wante...  2.88 us
    pallas_call x1, Pallas kernels, run_values(): pl.pallas_call(functools.partial(value_kernel, count, arrivals), out_shap...  2.61 us
    pallas_call x1, Pallas kernels, run_pack(): pl.pallas_call(pack_kernel, out_shape=[shaped((WIDE + NOTES, EMB), BF16),...  1.03 us
  transfers between devices with their start and end apart: 20, of which 9 were waited for; matrix products, arithmetic and copies ran while one was open for 1% of the time, Pallas kernels for 2%

profile of v4, /device:TPU:0, one launch (start us, length us, event | category | flops | bytes accessed | tf_op | source)
XLA Modules:
  0.0 46.9 jit_solution(15890660494217990599)
XLA Ops:
  0.6 5.1 %collective-permute-start.5 = (bf16[256,256]{1,0:T(8,128)(2,1)}, bf16[256,256]{1,0:T(8,128)(2,1)S(1)}, u32[]{:S(2)}, u32[]{:S(2)}) collective-permute-start(bf16[256,256]{1,0:T(8,128)(2,1)} %imp.1), channel_id=1, source_target_pairs={{0,12},{1,3},{2,14},{3,1},{4,8},{5,7},{6,10},{7,5},{8,4},{9,11},{1... | collective-permute-start | bytes 393224 | tf_op jit(solution)/shard_map/ppermute | solution.py:347
  5.8 0.0 collective-permute-start.3
  5.8 4.2 %collective-permute-done.5.refs_7_ = bf16[256,256]{1,0:T(8,128)(2,1)S(1)} collective-permute-done((bf16[256,256]{1,0:T(8,128)(2,1)}, bf16[256,256]{1,0:T(8,128)(2,1)S(1)}, u32[]{:S(2)}, u32[]{:S(2)}) %collective-permute-start.5) | collective-permute-done | bytes 131104 | tf_op jit(solution)/shard_map/ppermute | solution.py:347
  10.0 3.3 %collective-permute-start.9 = (bf16[256,256]{1,0:T(8,128)(2,1)S(1)}, bf16[256,256]{1,0:T(8,128)(2,1)S(1)}, u32[]{:S(2)}, u32[]{:S(2)}) collective-permute-start(bf16[256,256]{1,0:T(8,128)(2,1)S(1)} %collective-permute-done.5.refs_7_), channel_id=1, source_target_pairs={{0,2},{2,0},{4,6},{6,4},{8,10},{10,8},{12,14},{14,12},{16,18},{18,... | collective-permute-start | bytes 393224 | tf_op jit(solution)/shard_map/ppermute | solution.py:347
  13.3 1.0 %pack.1 = (bf16[272,256]{1,0:T(8,128)(2,1)S(1)}, bf16[256,256]{1,0:T(8,128)(2,1)S(1)}) custom-call(bf16[256,256]{1,0:T(8,128)(2,1)} %adv.1, s32[256]{0:T(256)} %allow.1, s32[1,8]{1,0:T(1,128)} %slots.1, bf16[256,256]{1,0:T(8,128)(2,1)} %imp.1), custom_call_target="tpu_custom_call" | custom-call | tf_op jit(solution)/shard_map/pack/pallas_call | solution.py:262
  14.4 2.9 %collective-permute-start.2 = (bf16[272,256]{1,0:T(8,128)(2,1)S(1)}, bf16[272,256]{1,0:T(8,128)(2,1)S(1)}, u32[]{:S(2)}, u32[]{:S(2)}) collective-permute-start(bf16[272,256]{1,0:T(8,128)(2,1)S(1)} %get-tuple-element.14.refs_0_), channel_id=1, source_target_pairs={{0,12},{1,13},{2,14},{3,15},{4,8},{5,9},{6,10},{7,11},{8,4},{9,5},... | collective-permute-start | bytes 417800 | tf_op jit(solution)/shard_map/ppermute | solution.py:347
  17.3 0.0 collective-permute-done.3.refs_5_
  17.3 1.1 %collective-permute-start.7 = (bf16[256,256]{1,0:T(8,128)(2,1)S(1)}, bf16[256,256]{1,0:T(8,128)(2,1)S(1)}, u32[]{:S(2)}, u32[]{:S(2)}) collective-permute-start(bf16[256,256]{1,0:T(8,128)(2,1)S(1)} %collective-permute-done.3.refs_5_), channel_id=1, source_target_pairs={{0,2},{1,3},{2,0},{3,1},{4,6},{5,7},{6,4},{7,5},{8,10},{9,11},{10,... | collective-permute-start | bytes 393224 | tf_op jit(solution)/shard_map/ppermute | solution.py:347
  18.4 0.0 collective-permute-done.9
  18.4 1.3 %collective-permute-start.10 = (bf16[256,256]{1,0:T(8,128)(2,1)S(1)}, bf16[256,256]{1,0:T(8,128)(2,1)S(1)}, u32[]{:S(2)}, u32[]{:S(2)}) collective-permute-start(bf16[256,256]{1,0:T(8,128)(2,1)S(1)} %collective-permute-done.9), channel_id=1, source_target_pairs={{0,1},{2,3},{4,5},{6,7},{8,9},{10,11},{12,13},{14,15},{16,17},{18,... | collective-permute-start | bytes 393224 | tf_op jit(solution)/shard_map/ppermute | solution.py:347
  19.7 2.1 %collective-permute-start.1 = (bf16[272,256]{1,0:T(8,128)(2,1)S(1)}, bf16[272,256]{1,0:T(8,128)(2,1)S(1)}, u32[]{:S(2)}, u32[]{:S(2)}) collective-permute-start(bf16[272,256]{1,0:T(8,128)(2,1)S(1)} %get-tuple-element.14.refs_0_), channel_id=1, source_target_pairs={{0,8},{1,9},{2,10},{3,11},{4,12},{5,13},{6,14},{7,15},{8,0},{9,1},... | collective-permute-start | bytes 417800 | tf_op jit(solution)/shard_map/ppermute | solution.py:347
  21.7 0.5 %collective-permute-start = (bf16[272,256]{1,0:T(8,128)(2,1)S(1)}, bf16[272,256]{1,0:T(8,128)(2,1)S(1)}, u32[]{:S(2)}, u32[]{:S(2)}) collective-permute-start(bf16[272,256]{1,0:T(8,128)(2,1)S(1)} %get-tuple-element.14.refs_0_), channel_id=1, source_target_pairs={{0,4},{1,5},{2,6},{3,7},{4,0},{5,1},{6,2},{7,3},{8,12},{9,13},{10,... | collective-permute-start | bytes 417800 | tf_op jit(solution)/shard_map/ppermute | solution.py:347
  22.2 0.6 %collective-permute-done.2.refs_3_ = bf16[272,256]{1,0:T(8,128)(2,1)S(1)} collective-permute-done((bf16[272,256]{1,0:T(8,128)(2,1)S(1)}, bf16[272,256]{1,0:T(8,128)(2,1)S(1)}, u32[]{:S(2)}, u32[]{:S(2)}) %collective-permute-start.2) | collective-permute-done | bytes 139296 | tf_op jit(solution)/shard_map/ppermute | solution.py:347
  22.8 0.0 collective-permute-start.6
  22.8 0.0 collective-permute-done.7.refs_9_
  22.8 0.5 %collective-permute-start.4 = (bf16[256,256]{1,0:T(8,128)(2,1)S(1)}, bf16[256,256]{1,0:T(8,128)(2,1)S(1)}, u32[]{:S(2)}, u32[]{:S(2)}) collective-permute-start(bf16[256,256]{1,0:T(8,128)(2,1)S(1)} %collective-permute-done.3.refs_5_), channel_id=1, source_target_pairs={{0,1},{1,0},{2,3},{3,2},{4,5},{5,4},{6,7},{7,6},{8,9},{9,8},{10,11... | collective-permute-start | bytes 393224 | tf_op jit(solution)/shard_map/ppermute | solution.py:347
  23.3 0.0 collective-permute-done.10
  23.3 0.1 collective-permute-start.8
  23.4 3.8 %collective-permute-done.1.refs_2_ = bf16[272,256]{1,0:T(8,128)(2,1)S(1)} collective-permute-done((bf16[272,256]{1,0:T(8,128)(2,1)S(1)}, bf16[272,256]{1,0:T(8,128)(2,1)S(1)}, u32[]{:S(2)}, u32[]{:S(2)}) %collective-permute-start.1) | collective-permute-done | bytes 139296 | tf_op jit(solution)/shard_map/ppermute | solution.py:347
  27.2 0.0 collective-permute-done.refs_1_
  27.2 0.0 collective-permute-done.6.refs_8_
  27.2 0.0 collective-permute-done.4.refs_6_
  27.2 0.0 collective-permute-done.8.refs_10_
  27.2 2.6 %shard_map.59 = (f32[32,128,128]{2,1,0:T(8,128)S(1)}, f32[8,128,128]{2,1,0:T(8,128)S(1)}, f32[8,128,128]{2,1,0:T(8,128)S(1)}, f32[16,128]{1,0:T(8,128)S(1)}, s32[8,128]{1,0:T(8,128)S(1)}) custom-call(bf16[272,256]{1,0:T(8,128)(2,1)S(1)} %get-tuple-element.14.refs_0_, bf16[272,256]{1,0:T(8,128)(2,1)S(1)} %collective-permute-done.refs_1_, ...), custom_call_target="tpu_custom_call" | custom-call | tf_op jit(solution)/shard_map/pallas_call | solution.py:299
  29.8 0.1 collective-permute-start.13
  29.9 1.9 %collective-permute-start.12 = (f32[16,128]{1,0:T(8,128)S(1)}, f32[16,128]{1,0:T(8,128)S(1)}, u32[]{:S(2)}, u32[]{:S(2)}) collective-permute-start(f32[16,128]{1,0:T(8,128)S(1)} %get-tuple-element.19.refs_3_), channel_id=1, source_target_pairs={{0,2},{1,3},{2,0},{3,1},{4,6},{5,7},{6,4},{7,5},{8,10},{9,11},{10,... | collective-permute-start | bytes 24584 | tf_op jit(solution)/shard_map/ppermute | solution.py:347
  31.8 0.0 collective-permute-start.11
  31.9 1.1 %collective-permute-done.13.refs_6_ = f32[16,128]{1,0:T(8,128)S(1)} collective-permute-done((f32[16,128]{1,0:T(8,128)S(1)}, f32[16,128]{1,0:T(8,128)S(1)}, u32[]{:S(2)}, u32[]{:S(2)}) %collective-permute-start.13) | collective-permute-done | bytes 8224 | tf_op jit(solution)/shard_map/ppermute | solution.py:347
  33.0 0.7 %collective-permute-done.12.refs_5_ = f32[16,128]{1,0:T(8,128)S(1)} collective-permute-done((f32[16,128]{1,0:T(8,128)S(1)}, f32[16,128]{1,0:T(8,128)S(1)}, u32[]{:S(2)}, u32[]{:S(2)}) %collective-permute-start.12) | collective-permute-done | bytes 8224 | tf_op jit(solution)/shard_map/ppermute | solution.py:347
  33.6 0.0 collective-permute-done.11.refs_4_
  33.6 1.5 %update.1 = (f32[8,128,128]{2,1,0:T(8,128)S(1)}, f32[16,128]{1,0:T(8,128)S(1)}, f32[32,128,128]{2,1,0:T(8,128)S(1)}) custom-call(s32[8,128]{1,0:T(8,128)S(1)} %get-tuple-element.16.refs_0_, f32[32,128,128]{2,1,0:T(8,128)S(1)} %get-tuple-element.17.refs_1_, f32[8,128,128]{2,1,0:T(8,128)S(1)} %get-tuple-element.18.refs_2_, ...), custom_call_target="tpu_custom_call" | custom-call | tf_op jit(solution)/shard_map/update/pallas_call | solution.py:322
  35.2 1.0 %collective-permute-start.16 = (f32[16,128]{1,0:T(8,128)S(1)}, f32[16,128]{1,0:T(8,128)S(1)}, u32[]{:S(2)}, u32[]{:S(2)}) collective-permute-start(f32[16,128]{1,0:T(8,128)S(1)} %get-tuple-element.21.refs_3_), channel_id=1, source_target_pairs={{0,3},{1,2},{2,1},{3,0},{4,7},{5,6},{6,5},{7,4},{8,11},{9,10},{10,... | collective-permute-start | bytes 24584 | tf_op jit(solution)/shard_map/ppermute | solution.py:347
  36.2 1.4 %collective-permute-start.15 = (f32[16,128]{1,0:T(8,128)S(1)}, f32[16,128]{1,0:T(8,128)S(1)}, u32[]{:S(2)}, u32[]{:S(2)}) collective-permute-start(f32[16,128]{1,0:T(8,128)S(1)} %get-tuple-element.21.refs_3_), channel_id=1, source_target_pairs={{0,2},{1,3},{2,0},{3,1},{4,6},{5,7},{6,4},{7,5},{8,10},{9,11},{10,... | collective-permute-start | bytes 24584 | tf_op jit(solution)/shard_map/ppermute | solution.py:347
  37.6 0.0 collective-permute-start.14
  37.6 0.7 %collective-permute-done.16.refs_6_ = f32[16,128]{1,0:T(8,128)S(1)} collective-permute-done((f32[16,128]{1,0:T(8,128)S(1)}, f32[16,128]{1,0:T(8,128)S(1)}, u32[]{:S(2)}, u32[]{:S(2)}) %collective-permute-start.16) | collective-permute-done | bytes 8224 | tf_op jit(solution)/shard_map/ppermute | solution.py:347
  38.3 1.5 %collective-permute-done.15.refs_5_ = f32[16,128]{1,0:T(8,128)S(1)} collective-permute-done((f32[16,128]{1,0:T(8,128)S(1)}, f32[16,128]{1,0:T(8,128)S(1)}, u32[]{:S(2)}, u32[]{:S(2)}) %collective-permute-start.15) | collective-permute-done | bytes 8224 | tf_op jit(solution)/shard_map/ppermute | solution.py:347
  39.8 0.0 collective-permute-done.14.refs_4_
  39.8 1.4 %last_update.1 = (f32[2,8,128]{2,1,0:T(8,128)S(1)}, f32[2,2,128]{2,1,0:T(2,128)S(1)}) custom-call(s32[8,128]{1,0:T(8,128)S(1)} %get-tuple-element.16.refs_0_, f32[32,128,128]{2,1,0:T(8,128)S(1)} %get-tuple-element.17.refs_1_, f32[8,128,128]{2,1,0:T(8,128)S(1)} %get-tuple-element.18.refs_2_, f32[16,128]{1,0:T(8,128)S(1)} %get-tuple-element.21.refs_3_, ...), custom_call_target="tpu_custom_call" | custom-call | tf_op jit(solution)/shard_map/last_update/pallas_call | solution.py:322
  41.2 0.2 collective-permute-start.17
  41.4 1.4 %collective-permute-start.19 = (f32[2,128]{1,0:T(2,128)S(1)}, f32[2,128]{1,0:T(2,128)S(1)}, u32[]{:S(2)}, u32[]{:S(2)}) collective-permute-start(f32[2,128]{1,0:T(2,128)S(1)} %get-tuple-element.27), channel_id=1, source_target_pairs={{0,3},{1,2},{2,1},{3,0},{4,7},{5,6},{6,5},{7,4},{8,11},{9,10},{10,... | collective-permute-start | bytes 3080 | tf_op jit(solution)/shard_map/ppermute | solution.py:347
  42.8 0.6 %collective-permute-start.18 = (f32[2,128]{1,0:T(2,128)S(1)}, f32[2,128]{1,0:T(2,128)S(1)}, u32[]{:S(2)}, u32[]{:S(2)}) collective-permute-start(f32[2,128]{1,0:T(2,128)S(1)} %get-tuple-element.27), channel_id=1, source_target_pairs={{0,2},{1,3},{2,0},{3,1},{4,6},{5,7},{6,4},{7,5},{8,10},{9,11},{10,... | collective-permute-start | bytes 3080 | tf_op jit(solution)/shard_map/ppermute | solution.py:347
  43.4 0.6 %reduce_sum.9 = f32[2,128]{1,0:T(2,128)} reduce(f32[2,8,128]{2,1,0:T(8,128)S(1)} %get-tuple-element.25, f32[]{:T(128)} %constant.2.clone.1), dimensions={1}, to_apply=%region_0.1 | reduce | flops 1792 | bytes 9220 | tf_op jit(solution)/shard_map/reduce_sum | solution.py:424
  44.0 0.0 collective-permute-done.17
  44.0 0.4 collective-permute-done.19
  44.4 2.0 %collective-permute-done.18 = f32[2,128]{1,0:T(2,128)S(1)} collective-permute-done((f32[2,128]{1,0:T(2,128)S(1)}, f32[2,128]{1,0:T(2,128)S(1)}, u32[]{:S(2)}, u32[]{:S(2)}) %collective-permute-start.18) | collective-permute-done | bytes 1056 | tf_op jit(solution)/shard_map/ppermute | solution.py:347
  46.4 0.6 %add_bitcast_fusion = f32[256]{0:T(256)} fusion(f32[2,128]{1,0:T(2,128)S(1)} %collective-permute-done.18, f32[2,128]{1,0:T(2,128)S(1)} %collective-permute-done.19, f32[2,128]{1,0:T(2,128)S(1)} %collective-permute-done.17, f32[2,2,128]{2,1,0:T(2,128)S(1)} %get-tuple-element.24), kind=kLoop, calls=%fused_computation.1 | loop fusion | flops 768 | bytes 5120 | tf_op jit(solution)/shard_map/reshape | solution.py:433
  (2 shorter events, 0.0 us)
Async XLA Ops:
  0.6 9.4 %collective-permute-start.5 = (bf16[256,256]{1,0:T(8,128)(2,1)}, bf16[256,256]{1,0:T(8,128)(2,1)S(1)}, u32[]{:S(2)}, u32[]{:S(2)}) collective-permute-start(bf16[256,256]{1,0:T(8,128)(2,1)} %imp.1), channel_id=1, source_target_pairs={{0,12},{1,3},{2,14},{3,1},{4,8},{5,7},{6,10},{7,5},{8,4},{9,11},{1... | collective-permute-start | bytes 393224 | tf_op jit(solution)/shard_map/ppermute | solution.py:347
  5.8 11.5 %collective-permute-start.3 = (bf16[256,256]{1,0:T(8,128)(2,1)}, bf16[256,256]{1,0:T(8,128)(2,1)S(1)}, u32[]{:S(2)}, u32[]{:S(2)}) collective-permute-start(bf16[256,256]{1,0:T(8,128)(2,1)} %imp.1), channel_id=1, source_target_pairs={{0,4},{1,9},{2,6},{3,11},{4,0},{5,13},{6,2},{7,15},{8,12},{9,1},{1... | collective-permute-start | bytes 393224 | tf_op jit(solution)/shard_map/ppermute | solution.py:347
  10.0 8.4 %collective-permute-start.9 = (bf16[256,256]{1,0:T(8,128)(2,1)S(1)}, bf16[256,256]{1,0:T(8,128)(2,1)S(1)}, u32[]{:S(2)}, u32[]{:S(2)}) collective-permute-start(bf16[256,256]{1,0:T(8,128)(2,1)S(1)} %collective-permute-done.5.refs_7_), channel_id=1, source_target_pairs={{0,2},{2,0},{4,6},{6,4},{8,10},{10,8},{12,14},{14,12},{16,18},{18,... | collective-permute-start | bytes 393224 | tf_op jit(solution)/shard_map/ppermute | solution.py:347
  14.4 8.4 %collective-permute-start.2 = (bf16[272,256]{1,0:T(8,128)(2,1)S(1)}, bf16[272,256]{1,0:T(8,128)(2,1)S(1)}, u32[]{:S(2)}, u32[]{:S(2)}) collective-permute-start(bf16[272,256]{1,0:T(8,128)(2,1)S(1)} %get-tuple-element.14.refs_0_), channel_id=1, source_target_pairs={{0,12},{1,13},{2,14},{3,15},{4,8},{5,9},{6,10},{7,11},{8,4},{9,5},... | collective-permute-start | bytes 417800 | tf_op jit(solution)/shard_map/ppermute | solution.py:347
  17.3 5.5 %collective-permute-start.7 = (bf16[256,256]{1,0:T(8,128)(2,1)S(1)}, bf16[256,256]{1,0:T(8,128)(2,1)S(1)}, u32[]{:S(2)}, u32[]{:S(2)}) collective-permute-start(bf16[256,256]{1,0:T(8,128)(2,1)S(1)} %collective-permute-done.3.refs_5_), channel_id=1, source_target_pairs={{0,2},{1,3},{2,0},{3,1},{4,6},{5,7},{6,4},{7,5},{8,10},{9,11},{10,... | collective-permute-start | bytes 393224 | tf_op jit(solution)/shard_map/ppermute | solution.py:347
  18.4 4.9 %collective-permute-start.10 = (bf16[256,256]{1,0:T(8,128)(2,1)S(1)}, bf16[256,256]{1,0:T(8,128)(2,1)S(1)}, u32[]{:S(2)}, u32[]{:S(2)}) collective-permute-start(bf16[256,256]{1,0:T(8,128)(2,1)S(1)} %collective-permute-done.9), channel_id=1, source_target_pairs={{0,1},{2,3},{4,5},{6,7},{8,9},{10,11},{12,13},{14,15},{16,17},{18,... | collective-permute-start | bytes 393224 | tf_op jit(solution)/shard_map/ppermute | solution.py:347
  19.7 7.5 %collective-permute-start.1 = (bf16[272,256]{1,0:T(8,128)(2,1)S(1)}, bf16[272,256]{1,0:T(8,128)(2,1)S(1)}, u32[]{:S(2)}, u32[]{:S(2)}) collective-permute-start(bf16[272,256]{1,0:T(8,128)(2,1)S(1)} %get-tuple-element.14.refs_0_), channel_id=1, source_target_pairs={{0,8},{1,9},{2,10},{3,11},{4,12},{5,13},{6,14},{7,15},{8,0},{9,1},... | collective-permute-start | bytes 417800 | tf_op jit(solution)/shard_map/ppermute | solution.py:347
  21.7 5.5 %collective-permute-start = (bf16[272,256]{1,0:T(8,128)(2,1)S(1)}, bf16[272,256]{1,0:T(8,128)(2,1)S(1)}, u32[]{:S(2)}, u32[]{:S(2)}) collective-permute-start(bf16[272,256]{1,0:T(8,128)(2,1)S(1)} %get-tuple-element.14.refs_0_), channel_id=1, source_target_pairs={{0,4},{1,5},{2,6},{3,7},{4,0},{5,1},{6,2},{7,3},{8,12},{9,13},{10,... | collective-permute-start | bytes 417800 | tf_op jit(solution)/shard_map/ppermute | solution.py:347
  22.8 4.4 %collective-permute-start.6 = (bf16[256,256]{1,0:T(8,128)(2,1)S(1)}, bf16[256,256]{1,0:T(8,128)(2,1)S(1)}, u32[]{:S(2)}, u32[]{:S(2)}) collective-permute-start(bf16[256,256]{1,0:T(8,128)(2,1)S(1)} %collective-permute-done.5.refs_7_), channel_id=1, source_target_pairs={{0,1},{1,0},{2,3},{3,2},{4,5},{5,4},{6,7},{7,6},{8,9},{9,8},{10,11... | collective-permute-start | bytes 393224 | tf_op jit(solution)/shard_map/ppermute | solution.py:347
  22.8 4.4 %collective-permute-start.4 = (bf16[256,256]{1,0:T(8,128)(2,1)S(1)}, bf16[256,256]{1,0:T(8,128)(2,1)S(1)}, u32[]{:S(2)}, u32[]{:S(2)}) collective-permute-start(bf16[256,256]{1,0:T(8,128)(2,1)S(1)} %collective-permute-done.3.refs_5_), channel_id=1, source_target_pairs={{0,1},{1,0},{2,3},{3,2},{4,5},{5,4},{6,7},{7,6},{8,9},{9,8},{10,11... | collective-permute-start | bytes 393224 | tf_op jit(solution)/shard_map/ppermute | solution.py:347
  23.3 3.9 %collective-permute-start.8 = (bf16[256,256]{1,0:T(8,128)(2,1)S(1)}, bf16[256,256]{1,0:T(8,128)(2,1)S(1)}, u32[]{:S(2)}, u32[]{:S(2)}) collective-permute-start(bf16[256,256]{1,0:T(8,128)(2,1)S(1)} %collective-permute-done.7.refs_9_), channel_id=1, source_target_pairs={{0,1},{1,0},{2,3},{3,2},{4,5},{5,4},{6,7},{7,6},{8,9},{9,8},{10,11... | collective-permute-start | bytes 393224 | tf_op jit(solution)/shard_map/ppermute | solution.py:347
  29.8 3.1 %collective-permute-start.13 = (f32[16,128]{1,0:T(8,128)S(1)}, f32[16,128]{1,0:T(8,128)S(1)}, u32[]{:S(2)}, u32[]{:S(2)}) collective-permute-start(f32[16,128]{1,0:T(8,128)S(1)} %get-tuple-element.19.refs_3_), channel_id=1, source_target_pairs={{0,3},{1,2},{2,1},{3,0},{4,7},{5,6},{6,5},{7,4},{8,11},{9,10},{10,... | collective-permute-start | bytes 24584 | tf_op jit(solution)/shard_map/ppermute | solution.py:347
  29.9 3.7 %collective-permute-start.12 = (f32[16,128]{1,0:T(8,128)S(1)}, f32[16,128]{1,0:T(8,128)S(1)}, u32[]{:S(2)}, u32[]{:S(2)}) collective-permute-start(f32[16,128]{1,0:T(8,128)S(1)} %get-tuple-element.19.refs_3_), channel_id=1, source_target_pairs={{0,2},{1,3},{2,0},{3,1},{4,6},{5,7},{6,4},{7,5},{8,10},{9,11},{10,... | collective-permute-start | bytes 24584 | tf_op jit(solution)/shard_map/ppermute | solution.py:347
  31.8 1.8 %collective-permute-start.11 = (f32[16,128]{1,0:T(8,128)S(1)}, f32[16,128]{1,0:T(8,128)S(1)}, u32[]{:S(2)}, u32[]{:S(2)}) collective-permute-start(f32[16,128]{1,0:T(8,128)S(1)} %get-tuple-element.19.refs_3_), channel_id=1, source_target_pairs={{0,1},{1,0},{2,3},{3,2},{4,5},{5,4},{6,7},{7,6},{8,9},{9,8},{10,11... | collective-permute-start | bytes 24584 | tf_op jit(solution)/shard_map/ppermute | solution.py:347
  35.2 3.1 %collective-permute-start.16 = (f32[16,128]{1,0:T(8,128)S(1)}, f32[16,128]{1,0:T(8,128)S(1)}, u32[]{:S(2)}, u32[]{:S(2)}) collective-permute-start(f32[16,128]{1,0:T(8,128)S(1)} %get-tuple-element.21.refs_3_), channel_id=1, source_target_pairs={{0,3},{1,2},{2,1},{3,0},{4,7},{5,6},{6,5},{7,4},{8,11},{9,10},{10,... | collective-permute-start | bytes 24584 | tf_op jit(solution)/shard_map/ppermute | solution.py:347
  36.2 3.7 %collective-permute-start.15 = (f32[16,128]{1,0:T(8,128)S(1)}, f32[16,128]{1,0:T(8,128)S(1)}, u32[]{:S(2)}, u32[]{:S(2)}) collective-permute-start(f32[16,128]{1,0:T(8,128)S(1)} %get-tuple-element.21.refs_3_), channel_id=1, source_target_pairs={{0,2},{1,3},{2,0},{3,1},{4,6},{5,7},{6,4},{7,5},{8,10},{9,11},{10,... | collective-permute-start | bytes 24584 | tf_op jit(solution)/shard_map/ppermute | solution.py:347
  37.6 2.2 %collective-permute-start.14 = (f32[16,128]{1,0:T(8,128)S(1)}, f32[16,128]{1,0:T(8,128)S(1)}, u32[]{:S(2)}, u32[]{:S(2)}) collective-permute-start(f32[16,128]{1,0:T(8,128)S(1)} %get-tuple-element.21.refs_3_), channel_id=1, source_target_pairs={{0,1},{1,0},{2,3},{3,2},{4,5},{5,4},{6,7},{7,6},{8,9},{9,8},{10,11... | collective-permute-start | bytes 24584 | tf_op jit(solution)/shard_map/ppermute | solution.py:347
  41.2 2.8 %collective-permute-start.17 = (f32[2,128]{1,0:T(2,128)S(1)}, f32[2,128]{1,0:T(2,128)S(1)}, u32[]{:S(2)}, u32[]{:S(2)}) collective-permute-start(f32[2,128]{1,0:T(2,128)S(1)} %get-tuple-element.26), channel_id=1, source_target_pairs={{0,1},{1,0},{2,3},{3,2},{4,5},{5,4},{6,7},{7,6},{8,9},{9,8},{10,11... | collective-permute-start | bytes 3080 | tf_op jit(solution)/shard_map/ppermute | solution.py:347
  41.4 3.0 %collective-permute-start.19 = (f32[2,128]{1,0:T(2,128)S(1)}, f32[2,128]{1,0:T(2,128)S(1)}, u32[]{:S(2)}, u32[]{:S(2)}) collective-permute-start(f32[2,128]{1,0:T(2,128)S(1)} %get-tuple-element.27), channel_id=1, source_target_pairs={{0,3},{1,2},{2,1},{3,0},{4,7},{5,6},{6,5},{7,4},{8,11},{9,10},{10,... | collective-permute-start | bytes 3080 | tf_op jit(solution)/shard_map/ppermute | solution.py:347
  42.8 3.6 %collective-permute-start.18 = (f32[2,128]{1,0:T(2,128)S(1)}, f32[2,128]{1,0:T(2,128)S(1)}, u32[]{:S(2)}, u32[]{:S(2)}) collective-permute-start(f32[2,128]{1,0:T(2,128)S(1)} %get-tuple-element.27), channel_id=1, source_target_pairs={{0,2},{1,3},{2,0},{3,1},{4,6},{5,7},{6,4},{7,5},{8,10},{9,11},{10,... | collective-permute-start | bytes 3080 | tf_op jit(solution)/shard_map/ppermute | solution.py:347
